TPU v7x, 128 devices: a whole 4x4x4 slice. The times are simulated.
128 devices in a mesh: ba: 16 (over x_lo, y, core), col: 8 (over x_hi, z).
Axes of the slice: x: 4 (x_hi: 2, x_lo: 2; x = x_hi * 2 + x_lo), y: 4, z: 4, core: 2. Of those that a mesh axis runs over, the one named last changes fastest.
Arguments:
- r_pairs: bfloat16 [1, 3, 512, 512], replicated, may hold values from -6 to 6
- w_tiles: bfloat16 [1, 3, 512, 512, 512], P(None, None, 'ba', 'col'), may hold values from -0.375 to 0.375
- virt_energy: float32 [512], replicated, may hold values from 0.3 to 3
- energy_shift: float32 [1], replicated, may hold values from -14 to -8
Outputs:
- sigma: float32 [1, 3, 512, 512], P(None, None, 'ba', 'col')
All inputs are finite; a program needn't handle non-finite values.
Results may differ from a plain program's by a relative error of at most 0.00077.
Values may be sent and summed in bfloat16 or wider, within the bound.
No kernel may reach another device: no remote copies, remote signals or barrier semaphores. Data moves between devices by JAX's collectives and lax.ppermute only.
A program may use at most 64 MiB of HBM per device.

v0:
```python
import jax
import jax.numpy as jnp
from jax import lax
from jax.sharding import PartitionSpec as P


def split_up(x, dim, devices):
    dims = x.shape
    tiles = x.reshape(*dims[:dim], devices, dims[dim] // devices, *dims[dim + 1 :])
    return jnp.moveaxis(tiles, dim, 0)


def sum_at_owner(x, axis, dim):
    tiles = split_up(x, dim, lax.axis_size(axis))
    arrived = lax.all_to_all(tiles, axis, split_axis=0, concat_axis=0, tiled=True)
    return arrived.sum(axis=0)


def on_device(r_pairs, w_tiles, virt_energy, energy_shift):
    width = w_tiles.shape[4]
    b_width = w_tiles.shape[2]
    c_width = w_tiles.shape[3]
    b_count = lax.axis_size("ba")
    c_count = lax.axis_size("col")
    b_start = lax.axis_index("ba") * b_width
    c_start = lax.axis_index("col") * c_width
    energy_b = lax.dynamic_slice_in_dim(virt_energy, b_start, b_width)
    energy_c = lax.dynamic_slice_in_dim(virt_energy, c_start, c_width)
    flat = w_tiles.reshape(1, 3, b_width * c_width, width)
    cubes = jnp.einsum("tmad,tmxd->tax", r_pairs, flat, preferred_element_type=jnp.float32)
    cubes = cubes.astype(jnp.bfloat16).reshape(1, width, b_width, c_width)
    slab = lax.all_to_all(cubes[:, :, None], ("ba", "col"), split_axis=1, concat_axis=2, tiled=True)
    a_part = slab.shape[1]
    slab = slab.reshape(1, a_part, b_count, c_count, b_width, c_width)
    slab = jnp.transpose(slab, (0, 1, 2, 4, 3, 5)).reshape(1, a_part, width, width)
    slab_sum = (slab.astype(jnp.float32) + jnp.swapaxes(slab, 2, 3).astype(jnp.float32)).astype(
        jnp.bfloat16
    )
    slab_sum = slab_sum.reshape(1, a_part, b_count, b_width, c_count, c_width)
    slab_sum = jnp.transpose(slab_sum, (0, 1, 2, 4, 3, 5)).reshape(
        1, a_part, b_count * c_count, b_width, c_width
    )
    summed_home = lax.all_to_all(
        slab_sum, ("ba", "col"), split_axis=2, concat_axis=1, tiled=True
    ).reshape(1, width, b_width, c_width)
    partner = lax.all_to_all(
        jnp.swapaxes(summed_home, 1, 2), "ba", split_axis=2, concat_axis=1, tiled=True
    )
    denominator = (
        energy_shift[:, None, None, None]
        - virt_energy[None, :, None, None]
        - energy_b[None, None, :, None]
        - energy_c[None, None, None, :]
    )
    combined = (summed_home.astype(jnp.float32) + partner.astype(jnp.float32)) / denominator
    combined = combined.astype(jnp.bfloat16).reshape(1, width, b_width * c_width)
    row_summed = sum_at_owner(
        jnp.einsum("tax,tmxd->atmd", combined, flat, preferred_element_type=jnp.float32), "ba", 0
    )
    owned = sum_at_owner(row_summed, "col", 3)
    return jnp.transpose(owned, (1, 2, 0, 3))


def solution(mesh):
    in_specs = (P(), P(None, None, "ba", "col", None), P(), P())
    out_specs = P(None, None, "ba", "col")
    return jax.shard_map(
        on_device, mesh=mesh, in_specs=in_specs, out_specs=out_specs, check_vma=False
    )
```

profile of v0, /device:TPU:0, one launch (start us, length us, event | category | flops | bytes accessed | tf_op | source)
XLA Modules:
  0.0 313.7 jit_solution(7437572068669963758)
XLA Ops:
  0.0 0.0 copy-start
  0.0 1.4 copy-done
  1.4 7.5 %bitcast_convert_fusion = bf16[512,2048]{1,0:T(8,128)(2,1)} fusion(bf16[3,2048,512]{2,1,0:T(8,128)(2,1)} %bitcast.89, bf16[1,3,512,512]{3,2,1,0:T(8,128)(2,1)S(1)} %copy-done), kind=kOutput, calls=%fused_computation.5 | convolution fusion | flops 3222274048 | bytes 9961472 | tf_op jit(solution)/shard_map/tmad,tmxd->tax/dot_general | solution.py:30
  8.9 3.9 %copy.34 = bf16[512,2048]{0,1:T(8,128)(2,1)} copy(bf16[512,2048]{1,0:T(8,128)(2,1)} %bitcast_convert_fusion) | data formatting | bytes 4194304 | tf_op jit(solution)/shard_map/convert_element_type | solution.py:31
  12.8 7.4 %copy.35 = bf16[1,512,1,32,64]{4,3,2,0,1:T(8,128)(2,1)} copy(bf16[1,512,1,32,64]{1,4,3,2,0:T(8,128)(2,1)} %bitcast.85) | data formatting | bytes 4194304 | tf_op jit(solution)/shard_map/broadcast_in_dim;reshape | solution.py:32
  20.2 7.6 %reshape.171 = bf16[128,2,4096]{2,1,0:T(2,128)(2,1)} reshape(bf16[512,1,1,32,64]{4,3,2,1,0:T(8,128)(2,1)} %bitcast.80) | data formatting | bytes 4194304
  27.8 40.2 %all_to_all.49 = bf16[128,2,4096]{2,1,0:T(2,128)(2,1)} all-to-all(bf16[128,2,4096]{2,1,0:T(2,128)(2,1)} %reshape.171), channel_id=1, replica_groups=mesh['ba'=16,'col'=8] {'ba','col'}, dimensions={0} | all-to-all | bytes 4194304 | tf_op jit(solution)/shard_map/all_to_all | solution.py:32
  68.1 7.8 %reshape.172 = bf16[512,1,1,32,64]{4,3,2,1,0:T(8,128)(2,1)} reshape(bf16[128,2,4096]{2,1,0:T(2,128)(2,1)} %all_to_all.49) | data formatting | bytes 4194304
  75.9 3.4 %convert_bitcast_fusion.1 = f32[1,4,128,1,32,64]{5,4,1,2,3,0:T(8,128)S(1)} fusion(bf16[1,128,4,1,32,64]{5,4,2,1,3,0:T(8,128)(2,1)} %bitcast.78), kind=kLoop, calls=%fused_computation.1 | loop fusion | flops 1048576 | bytes 6291456 | tf_op jit(solution)/shard_map/convert_element_type | solution.py:36
  79.3 1.3 copy.36
  80.6 11.3 %copy.37 = f32[1,4,16,32,8,64]{5,4,3,2,1,0:T(8,128)} copy(f32[1,4,16,32,8,64]{5,3,4,2,1,0:T(8,128)S(1)} %bitcast.77) | data formatting | bytes 8388608 | tf_op jit(solution)/shard_map/convert_element_type | solution.py:36
  92.0 7.5 %reshape.162 = f32[1,4,512,512]{3,2,1,0:T(8,128)} reshape(f32[1,4,16,32,8,64]{5,4,3,2,1,0:T(8,128)} %copy.37) | data formatting | bytes 8388608 | tf_op jit(solution)/shard_map/convert_element_type | solution.py:36
  99.4 5.2 %copy.38 = f32[1,4,512,512]{2,3,1,0:T(8,128)} copy(f32[1,4,512,512]{3,2,1,0:T(8,128)} %reshape.162) | data formatting | bytes 8388608 | tf_op jit(solution)/shard_map/convert_element_type | solution.py:36
  104.7 5.5 %fusion = bf16[1,4,512,512]{2,3,1,0:T(8,128)(2,1)} fusion(f32[1,4,512,512]{2,3,1,0:T(8,128)} %copy.38, f32[1,4,512,512]{3,2,1,0:T(8,128)} %reshape.162), kind=kLoop, calls=%fused_computation.4 | loop fusion | flops 2097152 | bytes 10485760 | tf_op jit(solution)/shard_map/convert_element_type | solution.py:36
  110.2 4.2 %copy.39 = bf16[1,4,512,512]{3,2,1,0:T(8,128)(2,1)} copy(bf16[1,4,512,512]{2,3,1,0:T(8,128)(2,1)} %fusion) | data formatting | bytes 4194304 | tf_op jit(solution)/shard_map/convert_element_type | solution.py:36
  114.4 6.2 %reshape.156 = bf16[1,4,16,32,8,64]{5,4,3,2,1,0:T(8,128)(2,1)} reshape(bf16[1,4,512,512]{3,2,1,0:T(8,128)(2,1)} %copy.39) | data formatting | bytes 4194304 | tf_op jit(solution)/shard_map/reshape | solution.py:39
  120.6 3.4 %copy.40 = bf16[1,4,16,8,32,64]{5,4,3,2,1,0:T(8,128)(2,1)S(1)} copy(bf16[1,4,16,8,32,64]{5,3,4,2,1,0:T(8,128)(2,1)} %bitcast.81) | data formatting | bytes 4194304 | tf_op jit(solution)/shard_map/transpose | solution.py:40
  124.0 3.3 %copy.49 = bf16[1,4,128,32,64]{4,3,1,0,2:T(8,128)(2,1)} copy(bf16[1,4,128,32,64]{4,3,2,1,0:T(8,128)(2,1)S(1)} %bitcast.82) | data formatting | bytes 4194304 | tf_op jit(solution)/shard_map/reshape | solution.py:40
  127.2 7.6 %reshape.173 = bf16[128,2,4096]{2,1,0:T(2,128)(2,1)} reshape(bf16[128,1,4,32,64]{4,3,2,1,0:T(8,128)(2,1)} %bitcast.83) | data formatting | bytes 4194304
  134.9 34.6 %all_to_all.50 = bf16[128,2,4096]{2,1,0:T(2,128)(2,1)} all-to-all(bf16[128,2,4096]{2,1,0:T(2,128)(2,1)} %reshape.173), channel_id=1, replica_groups=mesh['ba'=16,'col'=8] {'ba','col'}, dimensions={0} | all-to-all | bytes 4194304 | tf_op jit(solution)/shard_map/all_to_all | solution.py:43
  169.4 7.8 %reshape.174 = bf16[128,1,4,32,64]{4,3,2,1,0:T(8,128)(2,1)} reshape(bf16[128,2,4096]{2,1,0:T(2,128)(2,1)} %all_to_all.50) | data formatting | bytes 4194304
  177.2 7.5 %reshape.175 = bf16[16,2,32768]{2,1,0:T(2,128)(2,1)} reshape(bf16[512,1,32,64]{3,2,1,0:T(8,128)(2,1)} %bitcast.75) | data formatting | bytes 4194304
  184.8 4.7 %all-to-all-start.2 = ((bf16[16,2,32768]{2,1,0:T(2,128)(2,1)}), bf16[16,2,32768]{2,1,0:T(2,128)(2,1)}, u32[]{:S(2)}, u32[]{:S(2)}) async-start(bf16[16,2,32768]{2,1,0:T(2,128)(2,1)} %reshape.175), calls=%async_computation.2 | async-start | bytes 4194304 | tf_op jit(solution)/shard_map/all_to_all | solution.py:46
  189.5 0.1 dynamic_slice.7
  189.6 0.1 dynamic_slice.6
  190.3 0.1 sub.59
  190.4 0.2 broadcast_subtract_fusion
  190.6 27.4 %all-to-all-done.2 = bf16[16,2,32768]{2,1,0:T(2,128)(2,1)} async-done(((bf16[16,2,32768]{2,1,0:T(2,128)(2,1)}), bf16[16,2,32768]{2,1,0:T(2,128)(2,1)}, u32[]{:S(2)}, u32[]{:S(2)}) %all-to-all-start.2) | async-done | bytes 2097184 | tf_op jit(solution)/shard_map/all_to_all | solution.py:46
  218.1 7.4 %reshape.176 = bf16[512,1,32,64]{3,2,1,0:T(8,128)(2,1)} reshape(bf16[16,2,32768]{2,1,0:T(2,128)(2,1)} %all-to-all-done.2) | data formatting | bytes 4194304
  225.5 3.8 %copy.43 = bf16[1,32,512,64]{3,2,1,0:T(8,128)(2,1)S(1)} copy(bf16[1,32,512,64]{3,1,0,2:T(8,128)(2,1)} %bitcast.84) | data formatting | bytes 4194304 | tf_op jit(solution)/shard_map/all_to_all | solution.py:46
  229.3 1.2 convert_bitcast_fusion
  230.5 1.4 copy.44
  231.9 0.8 copy-done.2
  232.7 4.9 %divide_convert_fusion = bf16[1,128,4,1,32,64]{5,4,2,1,3,0:T(8,128)(2,1)} fusion(f32[1,128,4,1,32,64]{5,4,2,1,3,0:T(8,128)S(1)} %bitcast.76, f32[64]{0:T(128)S(1)} %dynamic_slice.7, f32[128,4,32]{2,1,0:T(4,128)S(1)} %broadcast_subtract_fusion, bf16[128,1,4,32,64]{4,3,2,1,0:T(8,128)(2,1)S(1)} %copy-done.2), kind=kLoop, calls=%fused_computation.2 | loop fusion | flops 5242880 | bytes 8454400 | tf_op jit(solution)/shard_map/convert_element_type | solution.py:56
  237.6 6.8 %reshape.169 = bf16[512,2048,1]{1,0,2:T(8,128)(2,1)} reshape(bf16[1,128,4,1,32,64]{5,4,2,1,3,0:T(8,128)(2,1)} %divide_convert_fusion) | data formatting | bytes 4194304 | tf_op jit(solution)/shard_map/convert_element_type | solution.py:56
  244.3 6.2 %fusion.2 = f32[512,3,512]{2,0,1:T(8,128)S(1)} fusion(bf16[512,2048,1]{1,0,2:T(8,128)(2,1)} %reshape.169, bf16[3,2048,512]{2,1,0:T(8,128)(2,1)} %bitcast.90), kind=kOutput, calls=%fused_computation.12 | convolution fusion | flops 3221225472 | bytes 11534336 | tf_op jit(solution)/shard_map/tax,tmxd->atmd/dot_general | solution.py:58
  250.6 0.5 copy.45
  251.1 0.0 copy-start.1
  251.1 44.0 %all_to_all.51 = f32[16,32,1,3,512]{4,1,3,2,0:T(8,128)} all-to-all(f32[16,32,1,3,512]{4,1,3,2,0:T(8,128)S(1)} %copy.45), channel_id=1, replica_groups=mesh['ba'=16,'col'=8] {'ba'}, dimensions={0} | all-to-all | bytes 6291456 | tf_op jit(solution)/shard_map/all_to_all | solution.py:15
  295.2 2.2 reduce_sum.20
  297.4 0.1 reshape.160
  297.5 0.1 copy.50
  297.6 0.2 reshape.177
  297.8 13.4 %all_to_all.52 = f32[8,1,6144]{2,1,0:T(1,128)S(1)} all-to-all(f32[8,1,6144]{2,1,0:T(1,128)S(1)} %reshape.177), channel_id=1, replica_groups=mesh['ba'=16,'col'=8] {'col'}, dimensions={0} | all-to-all | bytes 393216 | tf_op jit(solution)/shard_map/all_to_all | solution.py:15
  311.2 0.5 broadcast.64
  311.7 1.1 reduce.2
  312.8 0.2 reshape.178
  313.0 0.7 bitcast_reduce_fusion
  (5 shorter events, 0.0 us)
Async XLA Ops:
  0.0 1.4 copy-start
  177.2 12.2 %copy-start.3 = (f32[512]{0:T(512)S(1)}, f32[512]{0:T(512)}, u32[]{:S(2)}) copy-start(f32[512]{0:T(512)} %param.6) | copy-start | bytes 6148
  184.8 33.3 %all-to-all-start.2 = ((bf16[16,2,32768]{2,1,0:T(2,128)(2,1)}), bf16[16,2,32768]{2,1,0:T(2,128)(2,1)}, u32[]{:S(2)}, u32[]{:S(2)}) async-start(bf16[16,2,32768]{2,1,0:T(2,128)(2,1)} %reshape.175), calls=%async_computation.2 | async-start | bytes 4194304 | tf_op jit(solution)/shard_map/all_to_all | solution.py:46
  230.5 2.2 copy-start.2
  251.1 62.6 %copy-start.1 = (bf16[1,3,512,512]{3,2,1,0:T(8,128)(2,1)S(1)}, bf16[1,3,512,512]{3,2,1,0:T(8,128)(2,1)}, u32[]{:S(2)}) copy-start(bf16[1,3,512,512]{3,2,1,0:T(8,128)(2,1)} %param.4) | copy-start | bytes 4718596
where the time goes:
time: 316 us; the launch traced here: 314 us
  blocking collectives  132 us (42%)
  local copies, waits for them, and re-layouts  116 us (37%)
  waiting for transfers between devices  27.4 us (9%)
  other arithmetic  19.2 us (6%)
  matrix products  13.7 us (4%)
  starting transfers between devices  4.7 us (1%)
    all_to_all x2, blocking collectives, sum_at_owner(): lax.all_to_all(tiles, axis, split_axis=0, concat_axis=0, tiled=True)  57.5 us
    unnamed x16, local copies, waits for them, and re-layouts  48.3 us
    all_to_all x1, blocking collectives, on_device(): lax.all_to_all(cubes[:, :, None], ('ba', 'col'), split_axis=1, concat_axi...  40.2 us
    all_to_all x1, blocking collectives, on_device(): lax.all_to_all(slab_sum, ('ba', 'col'), split_axis=2, concat_axis=1, tile...  34.6 us
    all_to_all x1, waiting for transfers between devices, on_device(): lax.all_to_all(jnp.swapaxes(summed_home, 1, 2), 'ba', split_axis=2, conca...  27.4 us
    convert_element_type x4, local copies, waits for them, and re-layouts, on_device(): slab.astype(jnp.float32) + jnp.swapaxes(slab, 2, 3).astype(jnp.float32)  25.4 us
    dot_general x1, matrix products, on_device(): jnp.einsum('tmad,tmxd->tax', r_pairs, flat, preferred_element_type=jnp.fl...  7.47 us
    another operation x1, local copies, waits for them, and re-layouts, on_device(): cubes[:, :, None]  7.41 us
  transfers between devices with their start and end apart: 1, of which 1 were waited for; matrix products, arithmetic and copies ran while one was open for 0% of the time, Pallas kernels for 0%

commit v1 on v0

v1 whole, which is shorter than its diff:
```python
import jax
import jax.numpy as jnp
from jax import lax
from jax.experimental import pallas as pl
from jax.experimental.pallas import tpu as pltpu
from jax.sharding import PartitionSpec as P

F32 = jnp.float32
BF16 = jnp.bfloat16
VMEM_LIMIT = 56 * 1024 * 1024


def cube_kernel(r_ref, w_ref, out_ref):
    acc = None
    for m in range(3):
        rows = w_ref[m].reshape(512, 512)
        term = lax.dot_general(
            r_ref[m], rows, (((1,), (1,)), ((), ())), preferred_element_type=F32
        )
        acc = term if acc is None else acc + term
    out_ref[...] = acc.astype(BF16).reshape(16, 1, 32, 512)


def make_cubes(r_pairs, w):
    return pl.pallas_call(
        cube_kernel,
        grid=(2, 2),
        in_specs=[
            pl.BlockSpec((3, 512, 512), lambda h, s: (0, 0, 0)),
            pl.BlockSpec((3, 16, 32, 512), lambda h, s: (0, s, h, 0)),
        ],
        out_specs=pl.BlockSpec((16, 1, 32, 512), lambda h, s: (0, h, 0, s)),
        out_shape=jax.ShapeDtypeStruct((16, 2, 32, 1024), BF16),
        compiler_params=pltpu.CompilerParams(vmem_limit_bytes=VMEM_LIMIT),
        name="cubes",
    )(r_pairs, w)


def group_select(lane, bit, low, high):
    keep = (lane & bit) == 0
    first = jnp.where(keep, low, pltpu.roll(high, bit, 1))
    second = jnp.where(keep, pltpu.roll(low, 128 - bit, 1), high)
    return first, second


def combine_kernel(
    x_ref, u1_ref, u2_ref, u3_ref, perm_ref, ea_ref, eb_ref, ec_ref, w_ref, out_ref,
    stage_ref, swap_ref, comb_ref,
):
    perm = perm_ref[...]
    lane = lax.broadcasted_iota(jnp.int32, (8, 128), 1)
    eb = eb_ref[...]
    for k in range(4):
        u2 = jnp.dot(u2_ref[k].reshape(64, 1024), perm, preferred_element_type=F32)
        u3 = jnp.dot(u3_ref[k].reshape(64, 1024), perm, preferred_element_type=F32)
        shifted = ea_ref[k]
        for h in range(2):
            other = u1_ref[k, h].astype(F32) + u2[32 * h : 32 * h + 32]
            other = other.astype(BF16).astype(F32)
            for j in range(8):
                stage_ref[j] = other[:, 128 * j : 128 * j + 128]
            for j in range(8):
                g = [stage_ref[:, 4 * j + f, :] for f in range(4)]
                m0, m2 = group_select(lane, 64, g[0], g[2])
                m1, m3 = group_select(lane, 64, g[1], g[3])
                d0, d1 = group_select(lane, 32, m0, m1)
                d2, d3 = group_select(lane, 32, m2, m3)
                for e, d in enumerate((d0, d1, d2, d3)):
                    swap_ref[j, pl.ds(e, 8, stride=4), :] = d
            own = x_ref[k, h].astype(F32) + u3[32 * h : 32 * h + 32]
            own = own.astype(BF16).astype(F32)
            swapped = jnp.concatenate([swap_ref[j] for j in range(8)], axis=1)
            den = (shifted - eb) - ec_ref[h : h + 1]
            comb = ((own + swapped) / den).astype(BF16)
            comb_ref[32 * k : 32 * k + 32, 1024 * h : 1024 * h + 1024] = comb
    low = lax.broadcasted_iota(jnp.int32, (16, 128), 1) < 64
    for m in range(3):
        sig = None
        for h in range(2):
            rows = w_ref[m, :, 32 * h : 32 * h + 32, :].reshape(1024, 512)
            term = jnp.dot(
                comb_ref[:, 1024 * h : 1024 * h + 1024], rows, preferred_element_type=F32
            )
            sig = term if sig is None else sig + term
        for k in range(4):
            for t in range(4):
                top = sig[32 * k : 32 * k + 16, 128 * t : 128 * t + 128]
                bottom = sig[32 * k + 16 : 32 * k + 32, 128 * t : 128 * t + 128]
                even = jnp.where(low, top, pltpu.roll(bottom, 64, 1))
                odd = jnp.where(low, pltpu.roll(top, 64, 1), bottom)
                out_ref[k, 2 * t, 16 * m : 16 * m + 16, :] = even.astype(BF16)
                out_ref[k, 2 * t + 1, 16 * m : 16 * m + 16, :] = odd.astype(BF16)


def combine(x, u1, u2, u3, perm, ea, eb, ec, w):
    blocks = pl.BlockSpec((4, 2, 32, 1024), lambda s: (s, 0, 0, 0))

    def whole(shape):
        return pl.BlockSpec(shape, lambda s: (0,) * len(shape), pipeline_mode=pl.Buffered(1))

    return pl.pallas_call(
        combine_kernel,
        grid=(4,),
        in_specs=[
            blocks, blocks, blocks, blocks,
            whole((1024, 1024)),
            pl.BlockSpec((4, 32, 1), lambda s: (s, 0, 0)),
            whole((1, 1024)),
            whole((2, 1024)),
            whole((3, 32, 64, 512)),
        ],
        out_specs=pl.BlockSpec((4, 8, 48, 128), lambda s: (s, 0, 0, 0)),
        out_shape=jax.ShapeDtypeStruct((16, 8, 48, 128), BF16),
        scratch_shapes=[
            pltpu.VMEM((8, 32, 128), F32),
            pltpu.VMEM((8, 32, 128), F32),
            pltpu.VMEM((128, 2048), BF16),
        ],
        compiler_params=pltpu.CompilerParams(vmem_limit_bytes=VMEM_LIMIT),
        name="combine",
    )(x, u1, u2, u3, perm, ea, eb, ec, w)


def total_kernel(parts_ref, out_ref):
    total = parts_ref[0:8].astype(F32).sum(axis=0)
    for s in range(1, 16):
        total = total + parts_ref[8 * s : 8 * s + 8].astype(F32).sum(axis=0)
    for m in range(3):
        out_ref[m, 0:16, :] = total[16 * m : 16 * m + 16, 0:64]
        out_ref[m, 16:32, :] = total[16 * m : 16 * m + 16, 64:128]


def total_of(parts):
    return pl.pallas_call(
        total_kernel,
        out_shape=jax.ShapeDtypeStruct((3, 32, 64), F32),
        compiler_params=pltpu.CompilerParams(vmem_limit_bytes=VMEM_LIMIT),
        name="total",
    )(parts)


def exchange(x, axis):
    return lax.all_to_all(x, axis, split_axis=0, concat_axis=0, tiled=True)


def on_device(r_pairs, w_tiles, virt_energy, energy_shift):
    w = w_tiles[0]
    x = make_cubes(r_pairs[0], w)
    u1 = exchange(x, "ba")
    u2 = exchange(u1.reshape(8, 2, 2, 32, 1024), "col")
    u2 = jnp.swapaxes(u2, 1, 2).reshape(16, 2, 32, 1024)
    u3 = exchange(u2, "ba")
    perm = jnp.arange(1024)
    perm = ((perm % 32) * 32 + perm // 32)[:, None] == perm[None, :]
    b_start = lax.axis_index("ba") * 32
    c_start = lax.axis_index("col") * 64
    energy_b = lax.dynamic_slice_in_dim(virt_energy, b_start, 32)
    energy_c = lax.dynamic_slice_in_dim(virt_energy, c_start, 64)
    ea = (energy_shift - virt_energy).reshape(16, 32, 1)
    eb = jnp.broadcast_to(energy_b[:, None], (32, 32)).reshape(1, 1024)
    ec = jnp.broadcast_to(energy_c.reshape(2, 1, 32), (2, 32, 32)).reshape(2, 1024)
    parts = combine(x, u1, u2, u3, perm.astype(BF16), ea, eb, ec, w)
    arrived = exchange(parts.reshape(128, 48, 128), ("ba", "col"))
    return total_of(arrived)[None]


def solution(mesh):
    in_specs = (P(), P(None, None, "ba", "col", None), P(), P())
    out_specs = P(None, None, "ba", "col")
    return jax.shard_map(
        on_device, mesh=mesh, in_specs=in_specs, out_specs=out_specs, check_vma=False
    )
```

time: 316 us -> 166 us (0.53)
  local copies, waits for them, and re-layouts: 116 us -> 5.21 us
  blocking collectives: 132 us -> 98.7 us
  Pallas kernels: 0 us -> 31.9 us
  other arithmetic: 19.2 us -> 1.77 us
  matrix products: 13.7 us -> 0 us
  waiting for transfers between devices: 27.4 us -> 23.8 us
    unnamed x16 -> x6, local copies, waits for them, and re-layouts: 48.3 us -> 2.37 us
    convert_element_type x8 -> x0, local copies, waits for them, and re-layouts: 41.7 us -> none  [the longest x4 25.4 us: on_device(): slab.astype(jnp.float32) + jnp.swapaxes(slab, 2, 3).astype(jnp.float32)]
    all_to_all x4 -> x3, blocking collectives: 132 us -> 98.7 us  [exchange(): return lax.all_to_all(x, axis, split_axis=0, concat_axis=0, tiled=True)]
    pallas_call x0 -> x3, Pallas kernels: none -> 31.9 us  [the longest x1 22.1 us: combine(): pl.pallas_call(combine_kernel, grid=(4,), in_specs=[blocks, blocks, block...]
    dot_general x2 -> x0, matrix products: 13.7 us -> none  [the longest x1 7.47 us: on_device(): jnp.einsum('tmad,tmxd->tax', r_pairs, flat, preferred_element_type=jnp.fl...]
    convert_element_type x4 -> x1, other arithmetic: 15 us -> 1.76 us  [on_device(): parts = combine(x, u1, u2, u3, perm.astype(BF16), ea, eb, ec, w)]
    reshape x4, local copies, waits for them, and re-layouts: 10.1 us -> 2.53 us  [the longest x1 0.91 us: on_device(): ea = (energy_shift - virt_energy).reshape(16, 32, 1)]
    another operation x1 -> x0, local copies, waits for them, and re-layouts: 7.41 us -> none  [on_device(): cubes[:, :, None]]
  transfers between devices with their start and end apart: 1 -> 1, of which waited for: 1 -> 1; matrix products, arithmetic and copies ran while one was open for 0% -> 3% of each run, Pallas kernels for 0% -> 0%
where the time goes in v1:
time: 166 us
  blocking collectives  98.7 us (59%)
  Pallas kernels  31.9 us (19%)
  waiting for transfers between devices  23.8 us (14%)
  local copies, waits for them, and re-layouts  5.21 us (3%)
  starting transfers between devices  3.85 us (2%)
  other arithmetic  1.77 us (1%)
    all_to_all x3, blocking collectives, exchange(): return lax.all_to_all(x, axis, split_axis=0, concat_axis=0, tiled=True)  98.7 us
    all_to_all x1, waiting for transfers between devices, exchange(): return lax.all_to_all(x, axis, split_axis=0, concat_axis=0, tiled=True)  23.8 us
    pallas_call x1, Pallas kernels, combine(): pl.pallas_call(combine_kernel, grid=(4,), in_specs=[blocks, blocks, block...  22.1 us
    pallas_call x1, Pallas kernels, make_cubes(): pl.pallas_call(cube_kernel, grid=(2, 2), in_specs=[pl.BlockSpec((3, 512,...  7.53 us
    all_to_all x1, starting transfers between devices, exchange(): return lax.all_to_all(x, axis, split_axis=0, concat_axis=0, tiled=True)  3.85 us
  transfers between devices with their start and end apart: 1, of which 1 were waited for; matrix products, arithmetic and copies ran while one was open for 3% of the time, Pallas kernels for 0%

profile of v1, /device:TPU:0, one launch (start us, length us, event | category | flops | bytes accessed | tf_op | source)
XLA Modules:
  0.0 165.9 jit_solution(1065471722465738689)
XLA Ops:
  0.0 7.5 %cubes.1.x_ref = bf16[16,2,32,1024]{3,2,1,0:T(8,128)(2,1)} custom-call(bf16[3,512,512]{2,1,0:T(8,128)(2,1)} %bitcast.14, bf16[3,32,64,512]{3,2,1,0:T(8,128)(2,1)} %bitcast.10), custom_call_target="tpu_custom_call" | custom-call | tf_op jit(solution)/shard_map/cubes/pallas_call | solution.py:25
  7.5 33.3 %all_to_all.20.u1_ref = bf16[16,2,32,1024]{3,2,1,0:T(8,128)(2,1)S(1)} all-to-all(bf16[16,2,32,1024]{3,2,1,0:T(8,128)(2,1)} %cubes.1.x_ref), channel_id=1, replica_groups=mesh['ba'=16,'col'=8] {'ba'}, dimensions={0} | all-to-all | bytes 4194304 | tf_op jit(solution)/shard_map/all_to_all | solution.py:143
  40.8 0.0 copy-start
  40.8 0.3 copy.6
  41.1 1.0 copy-done
  42.1 35.3 %all_to_all.21 = bf16[8,2,2,32,1024]{4,3,1,2,0:T(8,128)(2,1)} all-to-all(bf16[8,2,2,32,1024]{4,3,1,2,0:T(8,128)(2,1)S(1)} %copy.6), channel_id=1, replica_groups=mesh['ba'=16,'col'=8] {'col'}, dimensions={0} | all-to-all | bytes 4194304 | tf_op jit(solution)/shard_map/all_to_all | solution.py:143
  77.4 0.0 copy-start.2
  77.4 3.8 %all-to-all-start.2 = ((bf16[16,2,32,1024]{3,2,1,0:T(8,128)(2,1)}), bf16[16,2,32,1024]{3,2,1,0:T(8,128)(2,1)S(1)}, u32[]{:S(2)}, u32[]{:S(2)}) async-start(bf16[16,2,32,1024]{3,2,1,0:T(8,128)(2,1)} %bitcast.4.u2_ref), calls=%async_computation.2 | async-start | bytes 4194304 | tf_op jit(solution)/shard_map/all_to_all | solution.py:143
  81.9 0.0 copy-done.2
  81.9 0.1 dynamic_slice.7
  82.0 0.1 dynamic_slice.6
  82.1 0.1 broadcast_in_dim.9
  82.2 0.1 broadcast_in_dim.8
  82.2 0.7 reshape.46.eb_ref
  82.9 0.7 reshape.47.ec_ref
  83.6 0.9 reshape.49.ea_ref
  84.5 1.8 %fusion.perm_ref = bf16[1024,1024]{1,0:T(8,128)(2,1)} fusion(s32[1024]{0:T(1024)S(1)} %fusion.7), kind=kLoop, calls=%fused_computation.1 | loop fusion | flops 2097152 | bytes 2101248 | tf_op jit(solution)/shard_map/convert_element_type | solution.py:162
  86.3 23.8 %all-to-all-done.2.u3_ref = bf16[16,2,32,1024]{3,2,1,0:T(8,128)(2,1)S(1)} async-done(((bf16[16,2,32,1024]{3,2,1,0:T(8,128)(2,1)}), bf16[16,2,32,1024]{3,2,1,0:T(8,128)(2,1)S(1)}, u32[]{:S(2)}, u32[]{:S(2)}) %all-to-all-start.2) | async-done | bytes 2097184 | tf_op jit(solution)/shard_map/all_to_all | solution.py:143
  110.1 0.0 copy-start.1
  110.1 1.3 copy-done.1
  111.4 22.1 %combine.1 = bf16[16,8,48,128]{3,2,1,0:T(8,128)(2,1)} custom-call(bf16[16,2,32,1024]{3,2,1,0:T(8,128)(2,1)} %cubes.1.x_ref, bf16[16,2,32,1024]{3,2,1,0:T(8,128)(2,1)} %copy-done, bf16[16,2,32,1024]{3,2,1,0:T(8,128)(2,1)} %bitcast.4.u2_ref, bf16[16,2,32,1024]{3,2,1,0:T(8,128)(2,1)} %copy-done.1, bf16[1024,1024]{1,0:T(8,128)(2,1)} %fusion.perm_ref, ...), custom_call_target="tpu_custom_call" | custom-call | tf_op jit(solution)/shard_map/combine/pallas_call | solution.py:101
  133.5 30.1 %all_to_all.22.parts_ref = bf16[128,48,128]{2,1,0:T(8,128)(2,1)} all-to-all(bf16[128,48,128]{2,1,0:T(8,128)(2,1)} %bitcast.13), channel_id=1, replica_groups=mesh['ba'=16,'col'=8] {'ba','col'}, dimensions={0} | all-to-all | bytes 3145728 | tf_op jit(solution)/shard_map/all_to_all | solution.py:143
  163.6 2.3 %total.1 = f32[3,32,64]{2,1,0:T(8,128)} custom-call(bf16[128,48,128]{2,1,0:T(8,128)(2,1)} %all_to_all.22.parts_ref), custom_call_target="tpu_custom_call" | custom-call | tf_op jit(solution)/shard_map/total/pallas_call | solution.py:134
  (3 shorter events, 0.0 us)
Async XLA Ops:
  40.8 1.3 copy-start
  77.4 4.5 %copy-start.2 = (f32[512]{0:T(512)S(1)}, f32[512]{0:T(512)}, u32[]{:S(2)}) copy-start(f32[512]{0:T(512)} %param.6) | copy-start | bytes 6148
  77.4 32.7 %all-to-all-start.2 = ((bf16[16,2,32,1024]{3,2,1,0:T(8,128)(2,1)}), bf16[16,2,32,1024]{3,2,1,0:T(8,128)(2,1)S(1)}, u32[]{:S(2)}, u32[]{:S(2)}) async-start(bf16[16,2,32,1024]{3,2,1,0:T(8,128)(2,1)} %bitcast.4.u2_ref), calls=%async_computation.2 | async-start | bytes 4194304 | tf_op jit(solution)/shard_map/all_to_all | solution.py:143
  110.1 1.3 copy-start.1

commit v2 on v1

--- a/solution.py
+++ b/solution.py
@@ -43,20 +43,13 @@
     return first, second
 
 
-def combine_kernel(
-    x_ref, u1_ref, u2_ref, u3_ref, perm_ref, ea_ref, eb_ref, ec_ref, w_ref, out_ref,
-    stage_ref, swap_ref, comb_ref,
-):
-    perm = perm_ref[...]
+def swap_kernel(u1_ref, u2_ref, perm_ref, out_ref, stage_ref, swap_ref):
     lane = lax.broadcasted_iota(jnp.int32, (8, 128), 1)
-    eb = eb_ref[...]
+    u2 = jnp.dot(u2_ref[...].reshape(256, 1024), perm_ref[...], preferred_element_type=F32)
     for k in range(4):
-        u2 = jnp.dot(u2_ref[k].reshape(64, 1024), perm, preferred_element_type=F32)
-        u3 = jnp.dot(u3_ref[k].reshape(64, 1024), perm, preferred_element_type=F32)
-        shifted = ea_ref[k]
         for h in range(2):
-            other = u1_ref[k, h].astype(F32) + u2[32 * h : 32 * h + 32]
-            other = other.astype(BF16).astype(F32)
+            row = 64 * k + 32 * h
+            other = u1_ref[k, h].astype(F32) + u2[row : row + 32]
             for j in range(8):
                 stage_ref[j] = other[:, 128 * j : 128 * j + 128]
             for j in range(8):
@@ -67,58 +60,83 @@
                 d2, d3 = group_select(lane, 32, m2, m3)
                 for e, d in enumerate((d0, d1, d2, d3)):
                     swap_ref[j, pl.ds(e, 8, stride=4), :] = d
-            own = x_ref[k, h].astype(F32) + u3[32 * h : 32 * h + 32]
-            own = own.astype(BF16).astype(F32)
-            swapped = jnp.concatenate([swap_ref[j] for j in range(8)], axis=1)
-            den = (shifted - eb) - ec_ref[h : h + 1]
-            comb = ((own + swapped) / den).astype(BF16)
-            comb_ref[32 * k : 32 * k + 32, 1024 * h : 1024 * h + 1024] = comb
-    low = lax.broadcasted_iota(jnp.int32, (16, 128), 1) < 64
-    for m in range(3):
-        sig = None
-        for h in range(2):
-            rows = w_ref[m, :, 32 * h : 32 * h + 32, :].reshape(1024, 512)
-            term = jnp.dot(
-                comb_ref[:, 1024 * h : 1024 * h + 1024], rows, preferred_element_type=F32
-            )
-            sig = term if sig is None else sig + term
-        for k in range(4):
-            for t in range(4):
-                top = sig[32 * k : 32 * k + 16, 128 * t : 128 * t + 128]
-                bottom = sig[32 * k + 16 : 32 * k + 32, 128 * t : 128 * t + 128]
-                even = jnp.where(low, top, pltpu.roll(bottom, 64, 1))
-                odd = jnp.where(low, pltpu.roll(top, 64, 1), bottom)
-                out_ref[k, 2 * t, 16 * m : 16 * m + 16, :] = even.astype(BF16)
-                out_ref[k, 2 * t + 1, 16 * m : 16 * m + 16, :] = odd.astype(BF16)
+            for j in range(8):
+                out_ref[k, h, :, 128 * j : 128 * j + 128] = swap_ref[j].astype(BF16)
 
 
-def combine(x, u1, u2, u3, perm, ea, eb, ec, w):
+def whole(shape):
+    return pl.BlockSpec(shape, lambda s: (0,) * len(shape), pipeline_mode=pl.Buffered(1))
+
+
+def swapped_sum(u1, u2, perm):
     blocks = pl.BlockSpec((4, 2, 32, 1024), lambda s: (s, 0, 0, 0))
+    return pl.pallas_call(
+        swap_kernel,
+        grid=(4,),
+        in_specs=[blocks, blocks, whole((1024, 1024))],
+        out_specs=blocks,
+        out_shape=jax.ShapeDtypeStruct((16, 2, 32, 1024), BF16),
+        scratch_shapes=[pltpu.VMEM((8, 32, 128), F32), pltpu.VMEM((8, 32, 128), F32)],
+        compiler_params=pltpu.CompilerParams(vmem_limit_bytes=16 * 1024 * 1024),
+        cost_estimate=pl.CostEstimate(
+            flops=2 * 1024**3, bytes_accessed=10 * 1024**2, transcendentals=0
+        ),
+        name="swapped_sum",
+    )(u1, u2, perm)
 
-    def whole(shape):
-        return pl.BlockSpec(shape, lambda s: (0,) * len(shape), pipeline_mode=pl.Buffered(1))
 
+def combine_kernel(x_ref, u3_ref, swapped_ref, perm_ref, ea_ref, eb_ref, ec_ref, w_ref, out_ref, comb_ref):
+    step = pl.program_id(0)
+    u3 = jnp.dot(u3_ref[...].reshape(256, 1024), perm_ref[...], preferred_element_type=F32)
+    eb = eb_ref[...]
+    for k in range(4):
+        shifted = ea_ref[k]
+        for h in range(2):
+            row = 64 * k + 32 * h
+            own = (x_ref[k, h].astype(F32) + u3[row : row + 32]).astype(BF16).astype(F32)
+            den = (shifted - eb) - ec_ref[h : h + 1]
+            comb = ((own + swapped_ref[k, h].astype(F32)) / den).astype(BF16)
+            comb_ref[step, 32 * k : 32 * k + 32, 1024 * h : 1024 * h + 1024] = comb
+
+    @pl.when(step == 3)
+    def _():
+        low = lax.broadcasted_iota(jnp.int32, (16, 128), 1) < 64
+        for m in range(3):
+            sig = None
+            for h in range(2):
+                rows = w_ref[m, :, 32 * h : 32 * h + 32, :].reshape(1024, 512)
+                left = comb_ref[:, :, 1024 * h : 1024 * h + 1024].reshape(512, 1024)
+                term = jnp.dot(left, rows, preferred_element_type=F32)
+                sig = term if sig is None else sig + term
+            for k in range(16):
+                for t in range(4):
+                    top = sig[32 * k : 32 * k + 16, 128 * t : 128 * t + 128]
+                    bottom = sig[32 * k + 16 : 32 * k + 32, 128 * t : 128 * t + 128]
+                    even = jnp.where(low, top, pltpu.roll(bottom, 64, 1))
+                    odd = jnp.where(low, pltpu.roll(top, 64, 1), bottom)
+                    out_ref[k, 2 * t, 16 * m : 16 * m + 16, :] = even.astype(BF16)
+                    out_ref[k, 2 * t + 1, 16 * m : 16 * m + 16, :] = odd.astype(BF16)
+
+
+def combine(x, u3, swapped, perm, ea, eb, ec, w):
+    blocks = pl.BlockSpec((4, 2, 32, 1024), lambda s: (s, 0, 0, 0))
     return pl.pallas_call(
         combine_kernel,
         grid=(4,),
         in_specs=[
-            blocks, blocks, blocks, blocks,
+            blocks, blocks, blocks,
             whole((1024, 1024)),
             pl.BlockSpec((4, 32, 1), lambda s: (s, 0, 0)),
             whole((1, 1024)),
             whole((2, 1024)),
             whole((3, 32, 64, 512)),
         ],
-        out_specs=pl.BlockSpec((4, 8, 48, 128), lambda s: (s, 0, 0, 0)),
+        out_specs=whole((16, 8, 48, 128)),
         out_shape=jax.ShapeDtypeStruct((16, 8, 48, 128), BF16),
-        scratch_shapes=[
-            pltpu.VMEM((8, 32, 128), F32),
-            pltpu.VMEM((8, 32, 128), F32),
-            pltpu.VMEM((128, 2048), BF16),
-        ],
+        scratch_shapes=[pltpu.VMEM((4, 128, 2048), BF16)],
         compiler_params=pltpu.CompilerParams(vmem_limit_bytes=VMEM_LIMIT),
         name="combine",
-    )(x, u1, u2, u3, perm, ea, eb, ec, w)
+    )(x, u3, swapped, perm, ea, eb, ec, w)
 
 
 def total_kernel(parts_ref, out_ref):
@@ -151,7 +169,7 @@
     u2 = jnp.swapaxes(u2, 1, 2).reshape(16, 2, 32, 1024)
     u3 = exchange(u2, "ba")
     perm = jnp.arange(1024)
-    perm = ((perm % 32) * 32 + perm // 32)[:, None] == perm[None, :]
+    perm = (((perm % 32) * 32 + perm // 32)[:, None] == perm[None, :]).astype(BF16)
     b_start = lax.axis_index("ba") * 32
     c_start = lax.axis_index("col") * 64
     energy_b = lax.dynamic_slice_in_dim(virt_energy, b_start, 32)
@@ -159,7 +177,8 @@
     ea = (energy_shift - virt_energy).reshape(16, 32, 1)
     eb = jnp.broadcast_to(energy_b[:, None], (32, 32)).reshape(1, 1024)
     ec = jnp.broadcast_to(energy_c.reshape(2, 1, 32), (2, 32, 32)).reshape(2, 1024)
-    parts = combine(x, u1, u2, u3, perm.astype(BF16), ea, eb, ec, w)
+    swapped = swapped_sum(u1, u2, perm)
+    parts = combine(x, u3, swapped, perm, ea, eb, ec, w)
     arrived = exchange(parts.reshape(128, 48, 128), ("ba", "col"))
     return total_of(arrived)[None]
 

time: 166 us -> 157 us (0.946)
  waiting for transfers between devices: 23.8 us -> 13.7 us
    all_to_all x1, waiting for transfers between devices: 23.8 us -> 13.7 us  [exchange(): return lax.all_to_all(x, axis, split_axis=0, concat_axis=0, tiled=True)]
    pallas_call x1, Pallas kernels: 22.1 us -> 12.9 us  [combine(): pl.pallas_call(combine_kernel, grid=(4,), in_specs=[blocks, blocks, block...]
    pallas_call x0 -> x1, Pallas kernels: none -> 8.48 us  [swapped_sum(): pl.pallas_call(swap_kernel, grid=(4,), in_specs=[blocks, blocks, whole((1...]
    unnamed x6 -> x10, local copies, waits for them, and re-layouts: 2.37 us -> 4 us
  transfers between devices with their start and end apart: 1 -> 1, of which waited for: 1 -> 1; matrix products, arithmetic and copies ran while one was open for 3% -> 2% of each run, Pallas kernels for 0% -> 5%
where the time goes in v2:
time: 157 us; the launch traced here: 156 us
  blocking collectives  98.7 us (63%)
  Pallas kernels  31.2 us (20%)
  waiting for transfers between devices  13.7 us (9%)
  local copies, waits for them, and re-layouts  6.85 us (4%)
  starting transfers between devices  4.57 us (3%)
    all_to_all x3, blocking collectives, exchange(): return lax.all_to_all(x, axis, split_axis=0, concat_axis=0, tiled=True)  98.7 us
    all_to_all x1, waiting for transfers between devices, exchange(): return lax.all_to_all(x, axis, split_axis=0, concat_axis=0, tiled=True)  13.7 us
    pallas_call x1, Pallas kernels, combine(): pl.pallas_call(combine_kernel, grid=(4,), in_specs=[blocks, blocks, block...  12.9 us
    pallas_call x1, Pallas kernels, swapped_sum(): pl.pallas_call(swap_kernel, grid=(4,), in_specs=[blocks, blocks, whole((1...  8.48 us
    pallas_call x1, Pallas kernels, make_cubes(): pl.pallas_call(cube_kernel, grid=(2, 2), in_specs=[pl.BlockSpec((3, 512,...  7.54 us
    all_to_all x1, starting transfers between devices, exchange(): return lax.all_to_all(x, axis, split_axis=0, concat_axis=0, tiled=True)  4.57 us
    unnamed x10, local copies, waits for them, and re-layouts  4 us
  transfers between devices with their start and end apart: 1, of which 1 were waited for; matrix products, arithmetic and copies ran while one was open for 2% of the time, Pallas kernels for 5%

profile of v2, /device:TPU:0, one launch (start us, length us, event | category | flops | bytes accessed | tf_op | source)
XLA Modules:
  0.0 156.2 jit_solution(12664981518234041699)
XLA Ops:
  0.0 7.5 %cubes.1.x_ref = bf16[16,2,32,1024]{3,2,1,0:T(8,128)(2,1)} custom-call(bf16[3,512,512]{2,1,0:T(8,128)(2,1)} %bitcast.14, bf16[3,32,64,512]{3,2,1,0:T(8,128)(2,1)} %bitcast.11), custom_call_target="tpu_custom_call" | custom-call | tf_op jit(solution)/shard_map/cubes/pallas_call | solution.py:25
  7.5 33.3 %all_to_all.20.u1_ref = bf16[16,2,32,1024]{3,2,1,0:T(8,128)(2,1)S(1)} all-to-all(bf16[16,2,32,1024]{3,2,1,0:T(8,128)(2,1)} %cubes.1.x_ref), channel_id=1, replica_groups=mesh['ba'=16,'col'=8] {'ba'}, dimensions={0} | all-to-all | bytes 4194304 | tf_op jit(solution)/shard_map/all_to_all | solution.py:161
  40.8 0.0 copy-start.1
  40.8 0.3 copy.6
  41.1 1.1 copy-done.1
  42.2 35.3 %all_to_all.21 = bf16[8,2,2,32,1024]{4,3,1,2,0:T(8,128)(2,1)} all-to-all(bf16[8,2,2,32,1024]{4,3,1,2,0:T(8,128)(2,1)S(1)} %copy.6), channel_id=1, replica_groups=mesh['ba'=16,'col'=8] {'col'}, dimensions={0} | all-to-all | bytes 4194304 | tf_op jit(solution)/shard_map/all_to_all | solution.py:161
  77.5 0.0 copy-start.4
  77.5 4.6 %all-to-all-start.2 = ((bf16[16,2,32,1024]{3,2,1,0:T(8,128)(2,1)}), bf16[16,2,32,1024]{3,2,1,0:T(8,128)(2,1)}, u32[]{:S(2)}, u32[]{:S(2)}) async-start(bf16[16,2,32,1024]{3,2,1,0:T(8,128)(2,1)} %bitcast.4.u2_ref), calls=%async_computation.2 | async-start | bytes 4194304 | tf_op jit(solution)/shard_map/all_to_all | solution.py:161
  82.0 0.0 copy-done.4
  82.1 0.1 dynamic_slice.7
  82.1 0.1 broadcast_in_dim.9
  82.2 0.7 reshape.47.ec_ref
  82.9 0.1 dynamic_slice.6
  83.0 0.1 broadcast_in_dim.8
  83.1 0.7 reshape.46.eb_ref
  84.4 0.9 reshape.49.ea_ref
  85.3 0.4 fusion.perm_ref
  85.7 0.0 copy-start.2
  85.7 1.6 %copy-done.2 = bf16[16,2,32,1024]{3,2,1,0:T(8,128)(2,1)S(1)} copy-done((bf16[16,2,32,1024]{3,2,1,0:T(8,128)(2,1)S(1)}, bf16[16,2,32,1024]{3,2,1,0:T(8,128)(2,1)}, u32[]{:S(2)}) %copy-start.2) | copy-done | bytes 2097176
  87.3 0.0 copy-start
  87.3 8.5 %swapped_sum.1.swapped_ref = bf16[16,2,32,1024]{3,2,1,0:T(8,128)(2,1)S(1)} custom-call(bf16[16,2,32,1024]{3,2,1,0:T(8,128)(2,1)S(1)} %copy-done.2, bf16[16,2,32,1024]{3,2,1,0:T(8,128)(2,1)} %bitcast.4.u2_ref, bf16[1024,1024]{1,0:T(8,128)(2,1)S(1)} %fusion.perm_ref), custom_call_target="tpu_custom_call" | custom-call | flops 2147483648 | bytes 10485760 | tf_op jit(solution)/shard_map/swapped_sum/pallas_call | solution.py:73
  95.8 0.0 copy-done
  95.8 0.0 copy-start.3
  95.8 1.3 copy-done.3
  97.2 13.7 %all-to-all-done.2.u3_ref = bf16[16,2,32,1024]{3,2,1,0:T(8,128)(2,1)} async-done(((bf16[16,2,32,1024]{3,2,1,0:T(8,128)(2,1)}), bf16[16,2,32,1024]{3,2,1,0:T(8,128)(2,1)}, u32[]{:S(2)}, u32[]{:S(2)}) %all-to-all-start.2) | async-done | bytes 2097184 | tf_op jit(solution)/shard_map/all_to_all | solution.py:161
  110.9 12.9 %combine.1 = bf16[16,8,48,128]{3,2,1,0:T(8,128)(2,1)} custom-call(bf16[16,2,32,1024]{3,2,1,0:T(8,128)(2,1)} %cubes.1.x_ref, bf16[16,2,32,1024]{3,2,1,0:T(8,128)(2,1)} %all-to-all-done.2.u3_ref, bf16[16,2,32,1024]{3,2,1,0:T(8,128)(2,1)} %copy-done.3, bf16[1024,1024]{1,0:T(8,128)(2,1)} %copy-done, f32[16,32,1]{2,1,0:T(8,128)} %reshape.49.ea_ref, ...), custom_call_target="tpu_custom_call" | custom-call | tf_op jit(solution)/shard_map/combine/pallas_call | solution.py:123
  123.8 30.1 %all_to_all.22.parts_ref = bf16[128,48,128]{2,1,0:T(8,128)(2,1)} all-to-all(bf16[128,48,128]{2,1,0:T(8,128)(2,1)} %bitcast.13), channel_id=1, replica_groups=mesh['ba'=16,'col'=8] {'ba','col'}, dimensions={0} | all-to-all | bytes 3145728 | tf_op jit(solution)/shard_map/all_to_all | solution.py:161
  153.9 2.3 %total.1 = f32[3,32,64]{2,1,0:T(8,128)} custom-call(bf16[128,48,128]{2,1,0:T(8,128)(2,1)} %all_to_all.22.parts_ref), custom_call_target="tpu_custom_call" | custom-call | tf_op jit(solution)/shard_map/total/pallas_call | solution.py:152
  (3 shorter events, 0.0 us)
Async XLA Ops:
  40.8 1.3 copy-start.1
  77.5 4.6 %copy-start.4 = (f32[512]{0:T(512)S(1)}, f32[512]{0:T(512)}, u32[]{:S(2)}) copy-start(f32[512]{0:T(512)} %param.6) | copy-start | bytes 6148
  77.5 33.4 %all-to-all-start.2 = ((bf16[16,2,32,1024]{3,2,1,0:T(8,128)(2,1)}), bf16[16,2,32,1024]{3,2,1,0:T(8,128)(2,1)}, u32[]{:S(2)}, u32[]{:S(2)}) async-start(bf16[16,2,32,1024]{3,2,1,0:T(8,128)(2,1)} %bitcast.4.u2_ref), calls=%async_computation.2 | async-start | bytes 4194304 | tf_op jit(solution)/shard_map/all_to_all | solution.py:161
  85.7 1.6 %copy-start.2 = (bf16[16,2,32,1024]{3,2,1,0:T(8,128)(2,1)S(1)}, bf16[16,2,32,1024]{3,2,1,0:T(8,128)(2,1)}, u32[]{:S(2)}) copy-start(bf16[16,2,32,1024]{3,2,1,0:T(8,128)(2,1)} %copy-done.1) | copy-start | bytes 6291460
  87.3 8.5 %copy-start = (bf16[1024,1024]{1,0:T(8,128)(2,1)}, bf16[1024,1024]{1,0:T(8,128)(2,1)S(1)}, u32[]{:S(2)}) copy-start(bf16[1024,1024]{1,0:T(8,128)(2,1)S(1)} %fusion.perm_ref) | copy-start | bytes 6291460
  95.8 1.3 copy-start.3

commit v3 on v0

v3 whole, which is shorter than its diff:
```python
import jax
import jax.numpy as jnp
from jax import lax
from jax.experimental import pallas as pl
from jax.experimental.pallas import tpu as pltpu
from jax.sharding import PartitionSpec as P

F32 = jnp.float32
BF16 = jnp.bfloat16
VMEM_LIMIT = 56 * 1024 * 1024


def lane_bits(g):
    lane = lax.broadcasted_iota(jnp.int32, (8, 128), 1)
    value = ((lane >> 2) & 7) ^ g
    return [((value >> t) & 1) == 1 for t in range(3)]


def butterfly(values, masks):
    for t, mask in enumerate(masks):
        bit = 1 << t
        values = [jnp.where(mask, values[k ^ bit], values[k]) for k in range(len(values))]
    return values


def halves(first, second, top):
    return (
        jnp.where(top, first, pltpu.roll(second, 4, 0)),
        jnp.where(top, pltpu.roll(first, 4, 0), second),
    )


def group_select(lane, bit, low, high):
    keep = (lane & bit) == 0
    first = jnp.where(keep, low, pltpu.roll(high, bit, 1))
    second = jnp.where(keep, pltpu.roll(low, 128 - bit, 1), high)
    return first, second


def whole(shape):
    return pl.BlockSpec(shape, lambda s: (0,) * len(shape), pipeline_mode=pl.Buffered(1))


def params(limit=VMEM_LIMIT):
    return pltpu.CompilerParams(vmem_limit_bytes=limit)


SMEM_SPEC = pl.BlockSpec(memory_space=pltpu.SMEM)


def cube_kernel(place_ref, r_ref, w_ref, out_ref, x_ref):
    step = pl.program_id(0)
    base = place_ref[0] ^ (2 * place_ref[1])
    top = lax.broadcasted_iota(jnp.int32, (8, 128), 0) < 4
    masks = lane_bits(0)
    for half in range(2):
        acc = None
        for m in range(3):
            rows = w_ref[m, :, 32 * half : 32 * half + 32, :].reshape(256, 512)
            term = lax.dot_general(
                r_ref[m], rows, (((1,), (1,)), ((), ())), preferred_element_type=F32
            )
            acc = term if acc is None else acc + term
        x_ref[half] = acc.reshape(16, 32, 256)

    @pl.loop(0, 16)
    def _(a_hi):
        h = a_hi ^ base
        for tile in range(2):
            lanes = slice(128 * tile, 128 * tile + 128)
            values = []
            for t in range(4):
                values += halves(
                    x_ref[0, a_hi, 8 * t : 8 * t + 8, lanes],
                    x_ref[1, a_hi ^ 1, 8 * t : 8 * t + 8, lanes],
                    top,
                )
            for k, value in enumerate(butterfly(values, masks)):
                g = k ^ (2 * step + tile)
                out_ref[8 * h + g, :, lanes] = value.astype(BF16)


def make_cubes(place, r_pairs, w):
    return pl.pallas_call(
        cube_kernel,
        grid=(4,),
        in_specs=[
            SMEM_SPEC,
            whole((3, 512, 512)),
            pl.BlockSpec((3, 8, 64, 512), lambda s: (0, s, 0, 0)),
        ],
        out_specs=pl.BlockSpec((128, 8, 256), lambda s: (0, 0, s)),
        out_shape=jax.ShapeDtypeStruct((128, 8, 1024), BF16),
        scratch_shapes=[pltpu.VMEM((2, 16, 32, 256), F32)],
        compiler_params=params(),
        name="cubes",
    )(place, r_pairs, w)


def owner_bits(h, c_h):
    row = lax.broadcasted_iota(jnp.int32, (8, 128), 0)
    value = (2 * row + c_h) ^ h
    return [((value >> t) & 1) == 1 for t in range(4)]


def denominator_kernel(place_ref, ea_ref, eb_ref, ec_ref, out_ref, part_ref):
    lanes = lane_bits(place_ref[1])

    @pl.loop(0, 8)
    def _(x):
        for c_h in range(2):
            rows = owner_bits(place_ref[0], c_h)
            for a_r in range(4):
                values = [jnp.full((8, 128), ea_ref[32 * k + 4 * x + a_r], F32) for k in range(16)]
                for k, value in enumerate(butterfly(values, rows)):
                    part_ref[x, k, c_h, a_r] = value

    @pl.loop(0, 16)
    def _(k):
        for c_h in range(2):
            ec = ec_ref[c_h]
            for a_r in range(4):
                values = [part_ref[x, k, c_h, a_r] for x in range(8)]
                for x, value in enumerate(butterfly(values, lanes)):
                    out_ref[x, k, c_h, a_r] = (value - eb_ref[x, k]) - ec


def denominators(place, ea, eb, ec):
    shape = (8, 16, 2, 4, 8, 128)
    return pl.pallas_call(
        denominator_kernel,
        grid=(1,),
        in_specs=[SMEM_SPEC, SMEM_SPEC, whole((8, 16, 1, 128)), whole((2, 8, 128))],
        out_specs=whole(shape),
        out_shape=jax.ShapeDtypeStruct(shape, F32),
        scratch_shapes=[pltpu.VMEM(shape, F32)],
        compiler_params=params(24 * 1024 * 1024),
        cost_estimate=pl.CostEstimate(
            flops=20 * 1024**2, bytes_accessed=20 * 1024**2, transcendentals=0
        ),
        name="denominators",
    )(place, ea, eb, ec)


def owner_kernel(place_ref, m_ref, perm_ref, den_ref, out_ref, mf_ref, mp_ref, s_ref, q_ref):
    lane = lax.broadcasted_iota(jnp.int32, (8, 128), 1)
    lanes = lane_bits(place_ref[1])
    for part in range(4):
        block = m_ref[32 * part : 32 * part + 32].reshape(256, 1024)
        moved = jnp.dot(block, perm_ref[...], preferred_element_type=F32)
        for x in range(8):
            column = slice(128 * x, 128 * x + 128)
            mp_ref[x, 2 * part : 2 * part + 2] = moved[:, column].reshape(2, 16, 8, 128)
            mf_ref[x, 4 * part : 4 * part + 4] = (
                m_ref[32 * part : 32 * part + 32, :, column].astype(F32).reshape(4, 8, 8, 128)
            )

    @pl.loop(0, 8)
    def _(pair):
        for odd in range(2):
            i = 2 * pair + odd
            for c_h in range(2):
                summed = []
                for a_r in range(4):
                    values = []
                    for x in range(8):
                        own = mf_ref[x, i, :, 4 * c_h + a_r, :]
                        moved = mp_ref[x, :, 8 * c_h + pair, 4 * odd + a_r, :]
                        value = (own + moved).astype(BF16).astype(F32)
                        s_ref[x, i, c_h, a_r] = value
                        values.append(value)
                    summed.append(butterfly(values, lanes))
                for x in range(8):
                    m0, m2 = group_select(lane, 64, summed[0][x], summed[2][x])
                    m1, m3 = group_select(lane, 64, summed[1][x], summed[3][x])
                    d0, d1 = group_select(lane, 32, m0, m1)
                    d2, d3 = group_select(lane, 32, m2, m3)
                    for e, d in enumerate((d0, d1, d2, d3)):
                        q_ref[x, i, c_h, e] = d

    @pl.loop(0, 8)
    def _(x):
        for c_h in range(2):
            rows = owner_bits(place_ref[0], c_h)
            for a_r in range(4):
                values = butterfly([q_ref[x, i, c_h, a_r] for i in range(16)], rows)
                for i in range(16):
                    total = s_ref[x, i, c_h, a_r] + values[i]
                    mf_ref[x, i, :, 4 * c_h + a_r, :] = total / den_ref[x, i, c_h, a_r]

    for x in range(8):
        out_ref[:, :, 128 * x : 128 * x + 128] = mf_ref[x].reshape(128, 8, 128).astype(BF16)


def combine_at_owner(place, m, perm, den):
    shape = (8, 16, 2, 4, 8, 128)
    return pl.pallas_call(
        owner_kernel,
        grid=(1,),
        in_specs=[SMEM_SPEC, whole((128, 8, 1024)), whole((1024, 1024)), whole(shape)],
        out_specs=whole((128, 8, 1024)),
        out_shape=jax.ShapeDtypeStruct((128, 8, 1024), BF16),
        scratch_shapes=[
            pltpu.VMEM((8, 16, 8, 8, 128), F32),
            pltpu.VMEM((8, 8, 16, 8, 128), F32),
            pltpu.VMEM(shape, F32),
            pltpu.VMEM(shape, F32),
        ],
        compiler_params=params(),
        name="combine_at_owner",
    )(place, m, perm, den)


def contract_kernel(place_ref, m_ref, w_ref, out_ref, comb_ref, sum_ref):
    step = pl.program_id(0)
    base = place_ref[0] ^ (2 * place_ref[1])
    top = lax.broadcasted_iota(jnp.int32, (8, 128), 0) < 4
    masks = lane_bits(0)

    @pl.loop(0, 16)
    def _(a_hi):
        h = a_hi ^ base
        for tile in range(2):
            lanes = slice(128 * tile, 128 * tile + 128)
            values = []
            for k in range(8):
                g = k ^ (2 * step + tile)
                values.append(m_ref[8 * h + g, :, lanes].astype(F32))
            values = butterfly(values, masks)
            for t in range(2):
                first = halves(values[4 * t], values[4 * t + 1], top)
                second = halves(values[4 * t + 2], values[4 * t + 3], top)
                for half in range(2):
                    rows = jnp.concatenate([first[half], second[half]], axis=0).astype(BF16)
                    comb_ref[half, a_hi ^ half, 16 * t : 16 * t + 16, lanes] = rows

    for m in range(3):
        term = None
        for half in range(2):
            rows = w_ref[m, :, 32 * half : 32 * half + 32, :].reshape(256, 512)
            left = comb_ref[half].reshape(512, 256)
            product = jnp.dot(left, rows, preferred_element_type=F32)
            term = product if term is None else term + product

        @pl.when(step == 0)
        def _(m=m, term=term):
            sum_ref[m] = term

        @pl.when(step > 0)
        def _(m=m, term=term):
            sum_ref[m] = sum_ref[m] + term

    @pl.when(step == 3)
    def _():
        low = lax.broadcasted_iota(jnp.int32, (16, 128), 1) < 64
        for m in range(3):
            for k in range(16):
                for t in range(4):
                    column = slice(128 * t, 128 * t + 128)
                    upper = sum_ref[m, 32 * k : 32 * k + 16, column]
                    lower = sum_ref[m, 32 * k + 16 : 32 * k + 32, column]
                    even = jnp.where(low, upper, pltpu.roll(lower, 64, 1))
                    odd = jnp.where(low, pltpu.roll(upper, 64, 1), lower)
                    out_ref[k, 2 * t, 16 * m : 16 * m + 16, :] = even.astype(BF16)
                    out_ref[k, 2 * t + 1, 16 * m : 16 * m + 16, :] = odd.astype(BF16)


def contract(place, m, w):
    return pl.pallas_call(
        contract_kernel,
        grid=(4,),
        in_specs=[
            SMEM_SPEC,
            pl.BlockSpec((128, 8, 256), lambda s: (0, 0, s)),
            pl.BlockSpec((3, 8, 64, 512), lambda s: (0, s, 0, 0)),
        ],
        out_specs=whole((16, 8, 48, 128)),
        out_shape=jax.ShapeDtypeStruct((16, 8, 48, 128), BF16),
        scratch_shapes=[pltpu.VMEM((2, 16, 32, 256), BF16), pltpu.VMEM((3, 512, 512), F32)],
        compiler_params=params(),
        name="contract",
    )(place, m, w)


def total_kernel(parts_ref, out_ref):
    total = parts_ref[0:8].astype(F32).sum(axis=0)
    for s in range(1, 16):
        total = total + parts_ref[8 * s : 8 * s + 8].astype(F32).sum(axis=0)
    for m in range(3):
        out_ref[m, 0:16, :] = total[16 * m : 16 * m + 16, 0:64]
        out_ref[m, 16:32, :] = total[16 * m : 16 * m + 16, 64:128]


def total_of(parts):
    return pl.pallas_call(
        total_kernel,
        out_shape=jax.ShapeDtypeStruct((3, 32, 64), F32),
        compiler_params=pltpu.CompilerParams(vmem_limit_bytes=VMEM_LIMIT),
        name="total",
    )(parts)


def exchange(x, axis):
    return lax.all_to_all(x, axis, split_axis=0, concat_axis=0, tiled=True)


def on_device(r_pairs, w_tiles, virt_energy, energy_shift):
    w = w_tiles[0]
    place = jnp.stack([lax.axis_index("ba"), lax.axis_index("col")]).astype(jnp.int32)
    cubes = make_cubes(place, r_pairs[0], w)
    met = exchange(cubes, ("ba", "col"))
    ea = energy_shift - virt_energy
    eb = jnp.broadcast_to(virt_energy.reshape(16, 8, 4, 1), (16, 8, 4, 32))
    eb = jnp.swapaxes(eb.reshape(16, 8, 1, 128), 0, 1)
    ec = jnp.broadcast_to(virt_energy.reshape(8, 2, 1, 32), (8, 2, 4, 32))
    ec = jnp.swapaxes(ec.reshape(8, 2, 128), 0, 1)
    den = denominators(place, ea, eb, ec)
    perm = jnp.arange(1024)
    perm = (((perm % 32) * 32 + perm // 32)[:, None] == perm[None, :]).astype(BF16)
    combined = combine_at_owner(place, met, perm, den)
    home = exchange(combined, ("ba", "col"))
    parts = contract(place, home, w)
    arrived = exchange(parts.reshape(128, 48, 128), ("ba", "col"))
    return total_of(arrived)[None]


def solution(mesh):
    in_specs = (P(), P(None, None, "ba", "col", None), P(), P())
    out_specs = P(None, None, "ba", "col")
    return jax.shard_map(
        on_device, mesh=mesh, in_specs=in_specs, out_specs=out_specs, check_vma=False
    )
```

time: 316 us -> 149 us (0.47)
  local copies, waits for them, and re-layouts: 116 us -> 3.98 us
  blocking collectives: 132 us -> 63.6 us
  Pallas kernels: 0 us -> 44.9 us
  other arithmetic: 19.2 us -> 2.33 us
  matrix products: 13.7 us -> 0 us
  starting transfers between devices: 4.7 us -> 11.1 us
  waiting for transfers between devices: 27.4 us -> 21.6 us
    all_to_all x4 -> x2, blocking collectives: 132 us -> 63.6 us  [exchange(): return lax.all_to_all(x, axis, split_axis=0, concat_axis=0, tiled=True)]
    unnamed x16 -> x8, local copies, waits for them, and re-layouts: 48.3 us -> 3.29 us
    pallas_call x0 -> x5, Pallas kernels: none -> 44.9 us  [the longest x1 20.4 us: combine_at_owner(): pl.pallas_call(owner_kernel, grid=(1,), in_specs=[SMEM_SPEC, whole((128,...]
    convert_element_type x8 -> x0, local copies, waits for them, and re-layouts: 41.7 us -> none  [the longest x4 25.4 us: on_device(): slab.astype(jnp.float32) + jnp.swapaxes(slab, 2, 3).astype(jnp.float32)]
    dot_general x2 -> x0, matrix products: 13.7 us -> none  [the longest x1 7.47 us: on_device(): jnp.einsum('tmad,tmxd->tax', r_pairs, flat, preferred_element_type=jnp.fl...]
    convert_element_type x4 -> x1, other arithmetic: 15 us -> 1.73 us  [on_device(): ((perm % 32 * 32 + perm // 32)[:, None] == perm[None, :]).astype(BF16)]
    reshape x4 -> x2, local copies, waits for them, and re-layouts: 10.1 us -> 0.28 us  [the longest x1 0.2 us: on_device(): eb = jnp.swapaxes(eb.reshape(16, 8, 1, 128), 0, 1)]
    another operation x1 -> x0, local copies, waits for them, and re-layouts: 7.41 us -> none  [on_device(): cubes[:, :, None]]
  transfers between devices with their start and end apart: 1 -> 1, of which waited for: 1 -> 1; matrix products, arithmetic and copies ran while one was open for 0% -> 2% of each run, Pallas kernels for 0% -> 2%
where the time goes in v3:
time: 149 us; the launch traced here: 148 us
  blocking collectives  63.6 us (43%)
  Pallas kernels  44.9 us (30%)
  waiting for transfers between devices  21.6 us (14%)
  starting transfers between devices  11.1 us (7%)
  local copies, waits for them, and re-layouts  3.98 us (3%)
  other arithmetic  2.33 us (2%)
    all_to_all x2, blocking collectives, exchange(): return lax.all_to_all(x, axis, split_axis=0, concat_axis=0, tiled=True)  63.6 us
    all_to_all x1, waiting for transfers between devices, exchange(): return lax.all_to_all(x, axis, split_axis=0, concat_axis=0, tiled=True)  21.6 us
    pallas_call x1, Pallas kernels, combine_at_owner(): pl.pallas_call(owner_kernel, grid=(1,), in_specs=[SMEM_SPEC, whole((128,...  20.4 us
    pallas_call x1, Pallas kernels, contract(): pl.pallas_call(contract_kernel, grid=(4,), in_specs=[SMEM_SPEC, pl.BlockS...  11.3 us
    all_to_all x1, starting transfers between devices, exchange(): return lax.all_to_all(x, axis, split_axis=0, concat_axis=0, tiled=True)  11.1 us
    pallas_call x1, Pallas kernels, make_cubes(): pl.pallas_call(cube_kernel, grid=(4,), in_specs=[SMEM_SPEC, whole((3, 512...  8.59 us
    unnamed x8, local copies, waits for them, and re-layouts  3.29 us
  transfers between devices with their start and end apart: 1, of which 1 were waited for; matrix products, arithmetic and copies ran while one was open for 2% of the time, Pallas kernels for 2%

profile of v3, /device:TPU:0, one launch (start us, length us, event | category | flops | bytes accessed | tf_op | source)
XLA Modules:
  0.0 148.3 jit_solution(687776708209632500)
XLA Ops:
  0.0 0.6 pad_add_fusion.place_ref
  0.6 8.6 %cubes.1 = bf16[128,8,1024]{2,1,0:T(8,128)(2,1)} custom-call(s32[2]{0:T(128)} %pad_add_fusion.place_ref, bf16[3,512,512]{2,1,0:T(8,128)(2,1)} %bitcast.19, bf16[3,32,64,512]{3,2,1,0:T(8,128)(2,1)} %bitcast.16), custom_call_target="tpu_custom_call" | custom-call | tf_op jit(solution)/shard_map/cubes/pallas_call | solution.py:84
  9.2 0.0 copy-start.3
  9.2 0.0 copy-start.1
  9.2 11.1 %all-to-all-start = ((bf16[128,8,1024]{2,1,0:T(8,128)(2,1)}), bf16[128,8,1024]{2,1,0:T(8,128)(2,1)S(1)}, u32[]{:S(2)}, u32[]{:S(2)}) async-start(bf16[128,8,1024]{2,1,0:T(8,128)(2,1)} %cubes.1), calls=%async_computation | async-start | bytes 4194304 | tf_op jit(solution)/shard_map/all_to_all | solution.py:304
  20.3 0.0 copy-done.3
  20.3 0.1 broadcast_in_dim.21
  20.4 0.1 broadcast_in_dim.19
  21.2 0.1 reshape.36
  21.3 0.2 broadcast_in_dim.20
  21.5 0.2 reshape.35
  21.7 0.0 copy-done.1
  21.7 2.3 %denominators.1.den_ref = f32[8,16,2,4,8,128]{5,4,3,2,1,0:T(8,128)S(1)} custom-call(s32[2]{0:T(128)S(1)} %copy-done.1, f32[512]{0:T(512)S(1)} %broadcast_subtract_fusion.ea_ref, f32[8,16,1,128]{3,2,1,0:T(1,128)S(1)} %bitcast.14, f32[2,8,128]{2,1,0:T(8,128)S(1)} %bitcast.15), custom_call_target="tpu_custom_call" | custom-call | flops 20971520 | bytes 20971520 | tf_op jit(solution)/shard_map/denominators/pallas_call | solution.py:130
  24.0 0.0 copy-start
  24.0 1.9 %copy-done = f32[8,16,2,4,8,128]{5,4,3,2,1,0:T(8,128)} copy-done((f32[8,16,2,4,8,128]{5,4,3,2,1,0:T(8,128)}, f32[8,16,2,4,8,128]{5,4,3,2,1,0:T(8,128)S(1)}, u32[]{:S(2)}) %copy-start) | copy-done | bytes 4194328
  26.0 1.7 %fusion.perm_ref = bf16[1024,1024]{1,0:T(8,128)(2,1)} fusion(s32[1024]{0:T(1024)S(1)} %fusion.7), kind=kLoop, calls=%fused_computation.1 | loop fusion | flops 2097152 | bytes 2101248 | tf_op jit(solution)/shard_map/convert_element_type | solution.py:319
  27.7 21.6 %all-to-all-done.m_ref = bf16[128,8,1024]{2,1,0:T(8,128)(2,1)S(1)} async-done(((bf16[128,8,1024]{2,1,0:T(8,128)(2,1)}), bf16[128,8,1024]{2,1,0:T(8,128)(2,1)S(1)}, u32[]{:S(2)}, u32[]{:S(2)}) %all-to-all-start) | async-done | bytes 2097184 | tf_op jit(solution)/shard_map/all_to_all | solution.py:304
  49.3 0.0 copy-start.2
  49.3 1.4 copy-done.2
  50.7 20.4 %combine_at_owner.1 = bf16[128,8,1024]{2,1,0:T(8,128)(2,1)} custom-call(s32[2]{0:T(128)} %pad_add_fusion.place_ref, bf16[128,8,1024]{2,1,0:T(8,128)(2,1)} %copy-done.2, bf16[1024,1024]{1,0:T(8,128)(2,1)} %fusion.perm_ref, f32[8,16,2,4,8,128]{5,4,3,2,1,0:T(8,128)} %copy-done), custom_call_target="tpu_custom_call" | custom-call | tf_op jit(solution)/shard_map/combine_at_owner/pallas_call | solution.py:197
  71.1 34.6 %all_to_all.15.m_ref = bf16[128,8,1024]{2,1,0:T(8,128)(2,1)} all-to-all(bf16[128,8,1024]{2,1,0:T(8,128)(2,1)} %combine_at_owner.1), channel_id=1, replica_groups=mesh['ba'=16,'col'=8] {'ba','col'}, dimensions={0} | all-to-all | bytes 4194304 | tf_op jit(solution)/shard_map/all_to_all | solution.py:304
  105.7 11.3 %contract.1 = bf16[16,8,48,128]{3,2,1,0:T(8,128)(2,1)} custom-call(s32[2]{0:T(128)} %pad_add_fusion.place_ref, bf16[128,8,1024]{2,1,0:T(8,128)(2,1)} %all_to_all.15.m_ref, bf16[3,32,64,512]{3,2,1,0:T(8,128)(2,1)} %bitcast.17), custom_call_target="tpu_custom_call" | custom-call | tf_op jit(solution)/shard_map/contract/pallas_call | solution.py:269
  116.9 29.0 %all_to_all.16.parts_ref = bf16[128,48,128]{2,1,0:T(8,128)(2,1)} all-to-all(bf16[128,48,128]{2,1,0:T(8,128)(2,1)} %bitcast.18), channel_id=1, replica_groups=mesh['ba'=16,'col'=8] {'ba','col'}, dimensions={0} | all-to-all | bytes 3145728 | tf_op jit(solution)/shard_map/all_to_all | solution.py:304
  146.0 2.3 %total.1 = f32[3,32,64]{2,1,0:T(8,128)} custom-call(bf16[128,48,128]{2,1,0:T(8,128)(2,1)} %all_to_all.16.parts_ref), custom_call_target="tpu_custom_call" | custom-call | tf_op jit(solution)/shard_map/total/pallas_call | solution.py:295
  (5 shorter events, 0.0 us)
Async XLA Ops:
  9.2 11.2 %copy-start.3 = (f32[512]{0:T(512)S(1)}, f32[512]{0:T(512)}, u32[]{:S(2)}) copy-start(f32[512]{0:T(512)} %param.6) | copy-start | bytes 6148
  9.2 12.6 %copy-start.1 = (s32[2]{0:T(128)S(1)}, s32[2]{0:T(128)}, u32[]{:S(2)}) copy-start(s32[2]{0:T(128)} %pad_add_fusion.place_ref) | copy-start | bytes 28
  9.2 40.1 %all-to-all-start = ((bf16[128,8,1024]{2,1,0:T(8,128)(2,1)}), bf16[128,8,1024]{2,1,0:T(8,128)(2,1)S(1)}, u32[]{:S(2)}, u32[]{:S(2)}) async-start(bf16[128,8,1024]{2,1,0:T(8,128)(2,1)} %cubes.1), calls=%async_computation | async-start | bytes 4194304 | tf_op jit(solution)/shard_map/all_to_all | solution.py:304
  24.0 1.9 %copy-start = (f32[8,16,2,4,8,128]{5,4,3,2,1,0:T(8,128)}, f32[8,16,2,4,8,128]{5,4,3,2,1,0:T(8,128)S(1)}, u32[]{:S(2)}) copy-start(f32[8,16,2,4,8,128]{5,4,3,2,1,0:T(8,128)S(1)} %denominators.1.den_ref) | copy-start | bytes 12582916
  49.3 1.4 copy-start.2

commit v4 on v3

v4 whole, which is shorter than its diff:
```python
import jax
import jax.numpy as jnp
import numpy as np
from jax import lax
from jax.experimental import pallas as pl
from jax.experimental.pallas import tpu as pltpu
from jax.sharding import PartitionSpec as P

F32 = jnp.float32
BF16 = jnp.bfloat16
VMEM_LIMIT = 24 * 1024 * 1024


def lane_bits(g):
    lane = lax.broadcasted_iota(jnp.int32, (8, 128), 1)
    value = ((lane >> 2) & 7) ^ g
    return [((value >> t) & 1) == 1 for t in range(3)]


def butterfly(values, masks):
    for t, mask in enumerate(masks):
        bit = 1 << t
        values = [jnp.where(mask, values[k ^ bit], values[k]) for k in range(len(values))]
    return values


def halves(first, second, top):
    return (
        jnp.where(top, first, pltpu.roll(second, 4, 0)),
        jnp.where(top, pltpu.roll(first, 4, 0), second),
    )


def group_select(lane, bit, low, high):
    keep = (lane & bit) == 0
    first = jnp.where(keep, low, pltpu.roll(high, bit, 1))
    second = jnp.where(keep, pltpu.roll(low, 128 - bit, 1), high)
    return first, second


def whole(shape):
    return pl.BlockSpec(shape, lambda s: (0,) * len(shape), pipeline_mode=pl.Buffered(1))


def params(limit=VMEM_LIMIT):
    return pltpu.CompilerParams(vmem_limit_bytes=limit)


SMEM_SPEC = pl.BlockSpec(memory_space=pltpu.SMEM)


def cube_kernel(r_ref, w_ref, out_ref, x_ref):
    step = pl.program_id(0)
    base = lax.axis_index("ba") ^ (2 * lax.axis_index("col"))
    top = lax.broadcasted_iota(jnp.int32, (8, 128), 0) < 4
    masks = lane_bits(0)
    for half in range(2):
        acc = None
        for m in range(3):
            rows = w_ref[m, :, 32 * half : 32 * half + 32, :].reshape(256, 512)
            term = lax.dot_general(
                r_ref[m], rows, (((1,), (1,)), ((), ())), preferred_element_type=F32
            )
            acc = term if acc is None else acc + term
        x_ref[half] = acc.reshape(16, 32, 256)

    @pl.loop(0, 16)
    def _(a_hi):
        h = a_hi ^ base
        for tile in range(2):
            lanes = slice(128 * tile, 128 * tile + 128)
            values = []
            for t in range(4):
                values += halves(
                    x_ref[0, a_hi, 8 * t : 8 * t + 8, lanes],
                    x_ref[1, a_hi ^ 1, 8 * t : 8 * t + 8, lanes],
                    top,
                )
            for k, value in enumerate(butterfly(values, masks)):
                g = k ^ (2 * step + tile)
                out_ref[8 * h + g, :, lanes] = value.astype(BF16)


def make_cubes(r_pairs, w):
    return pl.pallas_call(
        cube_kernel,
        grid=(4,),
        in_specs=[
            whole((3, 512, 512)),
            pl.BlockSpec((3, 8, 64, 512), lambda s: (0, s, 0, 0)),
        ],
        out_specs=pl.BlockSpec((128, 8, 256), lambda s: (0, 0, s)),
        out_shape=jax.ShapeDtypeStruct((128, 8, 1024), BF16),
        scratch_shapes=[pltpu.VMEM((2, 16, 32, 256), F32)],
        compiler_params=params(58 * 1024 * 1024),
        name="cubes",
    )(r_pairs, w)


def owner_bits(h, c_h):
    row = lax.broadcasted_iota(jnp.int32, (8, 128), 0)
    value = (2 * row + c_h) ^ h
    return [((value >> t) & 1) == 1 for t in range(4)]


def owner_kernel(
    energy_ref, ec_ref, m_ref, perm_ref, turn_ref, out_ref,
    mf_ref, mp_ref, part_ref, table_ref, eb_ref, s_ref, turned_ref, q_ref, comb_ref,
):
    h, g = lax.axis_index("ba"), lax.axis_index("col")
    lane = lax.broadcasted_iota(jnp.int32, (8, 128), 1)
    lanes = lane_bits(g)
    rows = [owner_bits(h, c_h) for c_h in range(2)]
    shift = energy_ref[512]

    @pl.loop(0, 4)
    def _(part):
        columns = pl.ds(pl.multiple_of(256 * part, 256), 256)
        moved = jnp.dot(
            m_ref[...].reshape(1024, 1024), perm_ref[:, columns], preferred_element_type=F32
        )
        for odd in range(2):
            x = 2 * part + odd
            for j in range(8):
                for i in range(16):
                    row = 8 * (8 * i + j)
                    mp_ref[x, pl.ds(129 * (row // 128) + row % 128, 8), :] = moved[
                        row : row + 8, 128 * odd : 128 * odd + 128
                    ]
                    column = pl.ds(pl.multiple_of(256 * part + 128 * odd, 128), 128)
                    mf_ref[x, i, 9 * j : 9 * j + 8, :] = m_ref[8 * i + j, :, column].astype(F32)
        for a_r in range(4):
            for odd in range(2):
                x = 2 * part + odd
                values = [
                    jnp.full((8, 128), shift - energy_ref[32 * i + 4 * x + a_r], F32)
                    for i in range(16)
                ]
                for i, value in enumerate(butterfly(values, rows[0])):
                    part_ref[x, i, a_r] = value
        for odd in range(2):
            x = 2 * part + odd
            for i in range(16):
                b = [jnp.full((1, 128), energy_ref[32 * i + 4 * x + r], F32) for r in range(4)]
                low = jnp.where(lane[0:1] < 32, b[0], b[1])
                high = jnp.where(lane[0:1] < 96, b[2], b[3])
                eb_ref[x, i : i + 1] = jnp.where(lane[0:1] < 64, low, high)

    @pl.loop(0, 8)
    def _(pair):
        for odd in range(2):
            i = 2 * pair + odd
            for a_r in range(4):
                sums = []
                for c_h in range(2):
                    sums.append([
                        mf_ref[x, i, pl.ds(4 * c_h + a_r, 8, stride=9), :]
                        + mp_ref[x, pl.ds(64 * c_h + 4 * i + a_r, 8, stride=129), :]
                        for x in range(8)
                    ])
                crossed = [butterfly(values, lanes) for values in sums]
                for x in range(8):
                    s_ref[x, i, a_r] = jnp.concatenate([sums[0][x], sums[1][x]], axis=0).astype(BF16)
                    turned_ref[x, i, :, 128 * a_r : 128 * a_r + 128] = jnp.concatenate(
                        [crossed[0][x], crossed[1][x]], axis=0
                    ).astype(BF16)
                values = butterfly([part_ref[x, i, a_r] for x in range(8)], lanes)
                for x in range(8):
                    table_ref[x, i, a_r] = values[x]

    for half in range(2):
        q_ref[...] = jnp.dot(
            turned_ref[...].reshape(2048, 512),
            turn_ref[:, 256 * half : 256 * half + 256],
            preferred_element_type=F32,
        ).reshape(8, 16, 16, 256)

        @pl.loop(0, 8)
        def _(x, half=half):
            for odd in range(2):
                a_r = 2 * half + odd
                for c_h in range(2):
                    values = [
                        q_ref[x, i, 8 * c_h : 8 * c_h + 8, 128 * odd : 128 * odd + 128]
                        for i in range(16)
                    ]
                    values = butterfly(values, rows[c_h])
                    for i in range(16):
                        total = s_ref[x, i, a_r, 8 * c_h : 8 * c_h + 8, :].astype(F32) + values[i]
                        den = (table_ref[x, i ^ c_h, a_r] - eb_ref[x, i : i + 1]) - ec_ref[c_h]
                        comb_ref[x, i, pl.ds(9 * (4 * c_h + a_r), 8), :] = total / den

    @pl.loop(0, 16)
    def _(i):
        for j in range(8):
            for x in range(8):
                value = comb_ref[x, i, pl.ds(j, 8, stride=9), :]
                out_ref[8 * i + j, :, 128 * x : 128 * x + 128] = value.astype(BF16)


VMEM_SPEC = pl.BlockSpec(memory_space=pltpu.VMEM)


def combine_at_owner(energy, ec, m):
    source = np.arange(1024)
    perm = ((source % 32) * 32 + source // 32)[:, None] == source[None, :]
    source = np.arange(512)
    turned = (source // 32 % 4) * 128 + (source // 128) * 32 + source % 32
    turn = turned[:, None] == source[None, :]
    return pl.pallas_call(
        owner_kernel,
        in_specs=[SMEM_SPEC, VMEM_SPEC, VMEM_SPEC, VMEM_SPEC, VMEM_SPEC],
        out_specs=VMEM_SPEC,
        out_shape=jax.ShapeDtypeStruct((128, 8, 1024), BF16),
        scratch_shapes=[
            pltpu.VMEM((8, 16, 72, 128), F32),
            pltpu.VMEM((8, 1032, 128), F32),
            pltpu.VMEM((8, 16, 4, 8, 128), F32),
            pltpu.VMEM((8, 16, 4, 8, 128), F32),
            pltpu.VMEM((8, 16, 128), F32),
            pltpu.VMEM((8, 16, 4, 16, 128), BF16),
            pltpu.VMEM((8, 16, 16, 512), BF16),
            pltpu.VMEM((8, 16, 16, 256), F32),
            pltpu.VMEM((8, 16, 72, 128), F32),
        ],
        compiler_params=params(40 * 1024 * 1024),
        name="combine_at_owner",
    )(energy, ec, m, jnp.asarray(perm, BF16), jnp.asarray(turn, BF16))


def contract_kernel(m_ref, w_ref, out_ref, comb_ref, sum_ref):
    step = pl.program_id(0)
    base = lax.axis_index("ba") ^ (2 * lax.axis_index("col"))
    top = lax.broadcasted_iota(jnp.int32, (8, 128), 0) < 4
    masks = lane_bits(0)

    @pl.loop(0, 16)
    def _(a_hi):
        h = a_hi ^ base
        for tile in range(2):
            lanes = slice(128 * tile, 128 * tile + 128)
            values = []
            for k in range(8):
                g = k ^ (2 * step + tile)
                values.append(m_ref[8 * h + g, :, lanes].astype(F32))
            values = butterfly(values, masks)
            for t in range(2):
                first = halves(values[4 * t], values[4 * t + 1], top)
                second = halves(values[4 * t + 2], values[4 * t + 3], top)
                for half in range(2):
                    rows = jnp.concatenate([first[half], second[half]], axis=0).astype(BF16)
                    comb_ref[half, a_hi ^ half, 16 * t : 16 * t + 16, lanes] = rows

    for m in range(3):
        term = None
        for half in range(2):
            rows = w_ref[m, :, 32 * half : 32 * half + 32, :].reshape(256, 512)
            left = comb_ref[half].reshape(512, 256)
            product = jnp.dot(left, rows, preferred_element_type=F32)
            term = product if term is None else term + product

        @pl.when(step == 0)
        def _(m=m, term=term):
            sum_ref[m] = term

        @pl.when(step > 0)
        def _(m=m, term=term):
            sum_ref[m] = sum_ref[m] + term

    @pl.when(step == 3)
    def _():
        low = lax.broadcasted_iota(jnp.int32, (16, 128), 1) < 64
        for m in range(3):
            for k in range(16):
                for t in range(4):
                    column = slice(128 * t, 128 * t + 128)
                    upper = sum_ref[m, 32 * k : 32 * k + 16, column]
                    lower = sum_ref[m, 32 * k + 16 : 32 * k + 32, column]
                    even = jnp.where(low, upper, pltpu.roll(lower, 64, 1))
                    odd = jnp.where(low, pltpu.roll(upper, 64, 1), lower)
                    out_ref[k, 2 * t, 16 * m : 16 * m + 16, :] = even.astype(BF16)
                    out_ref[k, 2 * t + 1, 16 * m : 16 * m + 16, :] = odd.astype(BF16)


def contract(m, w):
    return pl.pallas_call(
        contract_kernel,
        grid=(4,),
        in_specs=[
            pl.BlockSpec((128, 8, 256), lambda s: (0, 0, s)),
            pl.BlockSpec((3, 8, 64, 512), lambda s: (0, s, 0, 0)),
        ],
        out_specs=whole((16, 8, 48, 128)),
        out_shape=jax.ShapeDtypeStruct((16, 8, 48, 128), BF16),
        scratch_shapes=[pltpu.VMEM((2, 16, 32, 256), BF16), pltpu.VMEM((3, 512, 512), F32)],
        compiler_params=params(),
        name="contract",
    )(m, w)


def total_kernel(parts_ref, out_ref):
    total = parts_ref[0:8].astype(F32).sum(axis=0)
    for s in range(1, 16):
        total = total + parts_ref[8 * s : 8 * s + 8].astype(F32).sum(axis=0)
    for m in range(3):
        out_ref[m, 0:16, :] = total[16 * m : 16 * m + 16, 0:64]
        out_ref[m, 16:32, :] = total[16 * m : 16 * m + 16, 64:128]


def total_of(parts):
    return pl.pallas_call(
        total_kernel,
        out_shape=jax.ShapeDtypeStruct((3, 32, 64), F32),
        compiler_params=pltpu.CompilerParams(vmem_limit_bytes=VMEM_LIMIT),
        name="total",
    )(parts)


def exchange(x, axis):
    return lax.all_to_all(x, axis, split_axis=0, concat_axis=0, tiled=True)


def on_device(r_pairs, w_tiles, virt_energy, energy_shift):
    w = w_tiles[0]
    ec = jnp.broadcast_to(virt_energy.reshape(8, 2, 1, 32), (8, 2, 4, 32))
    ec = jnp.swapaxes(ec.reshape(8, 2, 128), 0, 1)
    energy = jnp.concatenate([virt_energy, jnp.broadcast_to(energy_shift, (128,))])
    cubes, ec, energy = lax.optimization_barrier((make_cubes(r_pairs[0], w), ec, energy))
    met = exchange(cubes, ("ba", "col"))
    combined = combine_at_owner(energy, ec, met)
    home = exchange(combined, ("ba", "col"))
    arrived = exchange(contract(home, w).reshape(128, 48, 128), ("ba", "col"))
    return total_of(arrived)[None]


def solution(mesh):
    in_specs = (P(), P(None, None, "ba", "col", None), P(), P())
    out_specs = P(None, None, "ba", "col")
    return jax.shard_map(
        on_device, mesh=mesh, in_specs=in_specs, out_specs=out_specs, check_vma=False
    )
```

time: 149 us -> 134 us (0.90)
  blocking collectives: 63.6 us -> 103 us
  waiting for transfers between devices: 21.6 us -> 0 us
  Pallas kernels: 44.9 us -> 28.9 us
  starting transfers between devices: 11.1 us -> 0 us
  local copies, waits for them, and re-layouts: 3.98 us -> 1.56 us
  other arithmetic: 2.33 us -> 0.01 us
    all_to_all x2 -> x3, blocking collectives: 63.6 us -> 103 us  [exchange(): return lax.all_to_all(x, axis, split_axis=0, concat_axis=0, tiled=True)]
    all_to_all x1 -> x0, waiting for transfers between devices: 21.6 us -> none  [exchange(): return lax.all_to_all(x, axis, split_axis=0, concat_axis=0, tiled=True)]
    pallas_call x4 -> x3, Pallas kernels: 42.6 us -> 28 us  [the longest x1 10.1 us: combine_at_owner(): pl.pallas_call(owner_kernel, in_specs=[SMEM_SPEC, VMEM_SPEC, VMEM_SPEC, V...]
    all_to_all x1 -> x0, starting transfers between devices: 11.1 us -> none  [exchange(): return lax.all_to_all(x, axis, split_axis=0, concat_axis=0, tiled=True)]
    unnamed x8, local copies, waits for them, and re-layouts: 3.29 us -> 0.01 us
    convert_element_type x1 -> x0, other arithmetic: 1.73 us -> none  [on_device(): ((perm % 32 * 32 + perm // 32)[:, None] == perm[None, :]).astype(BF16)]
  transfers between devices with their start and end apart: 1 -> 0, of which waited for: 1 -> 0; matrix products, arithmetic and copies ran while one was open for 2% -> 0% of each run, Pallas kernels for 2% -> 0%
where the time goes in v4:
time: 134 us
  blocking collectives  103 us (77%)
  Pallas kernels  28.9 us (22%)
  local copies, waits for them, and re-layouts  1.56 us (1%)
    all_to_all x3, blocking collectives, exchange(): return lax.all_to_all(x, axis, split_axis=0, concat_axis=0, tiled=True)  103 us
    pallas_call x1, Pallas kernels, combine_at_owner(): pl.pallas_call(owner_kernel, in_specs=[SMEM_SPEC, VMEM_SPEC, VMEM_SPEC, V...  10.1 us
    pallas_call x1, Pallas kernels, contract(): pl.pallas_call(contract_kernel, grid=(4,), in_specs=[pl.BlockSpec((128, 8...  9.17 us
    pallas_call x1, Pallas kernels, make_cubes(): pl.pallas_call(cube_kernel, grid=(4,), in_specs=[whole((3, 512, 512)), pl...  8.74 us

profile of v4, /device:TPU:0, one launch (start us, length us, event | category | flops | bytes accessed | tf_op | source)
XLA Modules:
  0.0 134.1 jit_solution(11191886567625543087)
XLA Ops:
  0.7 0.8 broadcast_in_dim.15
  1.4 0.7 concatenate.3.energy_ref
  2.1 0.1 reshape.8
  2.2 0.0 copy-start
  2.2 0.0 copy-start.1
  2.2 8.7 %cubes.1 = bf16[128,8,1024]{2,1,0:T(8,128)(2,1)} custom-call(bf16[3,512,512]{2,1,0:T(8,128)(2,1)} %bitcast.15, bf16[3,32,64,512]{3,2,1,0:T(8,128)(2,1)} %bitcast.9), custom_call_target="tpu_custom_call" | custom-call | tf_op jit(solution)/shard_map/cubes/pallas_call | solution.py:85
  10.9 0.0 slice-start
  10.9 40.1 %all_to_all.15.m_ref = bf16[128,8,1024]{2,1,0:T(8,128)(2,1)S(1)} all-to-all(bf16[128,8,1024]{2,1,0:T(8,128)(2,1)} %cubes.1), channel_id=1, replica_groups=mesh['ba'=16,'col'=8] {'ba','col'}, dimensions={0} | all-to-all | bytes 4194304 | tf_op jit(solution)/shard_map/all_to_all | solution.py:320
  51.1 0.0 copy-done
  51.1 0.0 copy-done.1
  51.1 0.0 slice-start.1
  51.1 10.1 %combine_at_owner.1 = bf16[128,8,1024]{2,1,0:T(8,128)(2,1)S(1)} custom-call(f32[640]{0:T(1024)S(1)} %concatenate.3.energy_ref, f32[2,8,128]{2,1,0:T(8,128)S(1)} %bitcast.14, bf16[128,8,1024]{2,1,0:T(8,128)(2,1)S(1)} %all_to_all.15.m_ref, bf16[1024,1024]{1,0:T(8,128)(2,1)S(1)} %copy-done, bf16[512,512]{1,0:T(8,128)(2,1)S(1)} %copy-done.1), custom_call_target="tpu_custom_call" | custom-call | tf_op jit(solution)/shard_map/combine_at_owner/pallas_call | solution.py:210
  61.2 34.2 %all_to_all.16.m_ref = bf16[128,8,1024]{2,1,0:T(8,128)(2,1)S(1)} all-to-all(bf16[128,8,1024]{2,1,0:T(8,128)(2,1)S(1)} %combine_at_owner.1), channel_id=1, replica_groups=mesh['ba'=16,'col'=8] {'ba','col'}, dimensions={0} | all-to-all | bytes 4194304 | tf_op jit(solution)/shard_map/all_to_all | solution.py:320
  95.4 0.0 slice-done
  95.4 0.0 slice-done.1
  95.4 9.2 %contract.1 = bf16[16,8,48,128]{3,2,1,0:T(8,128)(2,1)S(1)} custom-call(bf16[128,8,1024]{2,1,0:T(8,128)(2,1)S(1)} %all_to_all.16.m_ref, bf16[3,32,64,512]{3,2,1,0:T(8,128)(2,1)S(1)} %bitcast.12), custom_call_target="tpu_custom_call" | custom-call | tf_op jit(solution)/shard_map/contract/pallas_call | solution.py:286
  104.6 28.6 %all_to_all.17.parts_ref = bf16[128,48,128]{2,1,0:T(8,128)(2,1)S(1)} all-to-all(bf16[128,48,128]{2,1,0:T(8,128)(2,1)S(1)} %bitcast.13), channel_id=1, replica_groups=mesh['ba'=16,'col'=8] {'ba','col'}, dimensions={0} | all-to-all | bytes 3145728 | tf_op jit(solution)/shard_map/all_to_all | solution.py:320
  133.2 0.9 total.1
  (3 shorter events, 0.0 us)
Async XLA Ops:
  2.2 48.9 %copy-start = (bf16[1024,1024]{1,0:T(8,128)(2,1)S(1)}, bf16[1024,1024]{1,0:T(8,128)(2,1)}, u32[]{:S(2)}) copy-start(bf16[1024,1024]{1,0:T(8,128)(2,1)} %constant.4.clone.perm_ref) | copy-start | bytes 6291460
  2.2 48.9 %copy-start.1 = (bf16[512,512]{1,0:T(8,128)(2,1)S(1)}, bf16[512,512]{1,0:T(8,128)(2,1)}, u32[]{:S(2)}) copy-start(bf16[512,512]{1,0:T(8,128)(2,1)} %constant.5.clone.turn_ref) | copy-start | bytes 1572868
  10.9 84.5 %slice-start = ((s8[6291456]{0:T(1024)(128)(4,1)}), s8[4194304]{0:T(1024)(128)(4,1)S(1)}, s32[]{:S(2)}) async-start(s8[6291456]{0:T(1024)(128)(4,1)} %bitcast.10), calls=%async_computation.3 | async-start | bytes 8388608
  51.1 44.3 %slice-start.1 = ((s8[6291456]{0:T(1024)(128)(4,1)}), s8[2097152]{0:T(1024)(128)(4,1)S(1)}, s32[]{:S(2)}) async-start(s8[6291456]{0:T(1024)(128)(4,1)} %bitcast.10), calls=%async_computation.4 | async-start | bytes 4194304

commit v5 on v4

--- a/solution.py
+++ b/solution.py
@@ -4,11 +4,21 @@
 from jax import lax
 from jax.experimental import pallas as pl
 from jax.experimental.pallas import tpu as pltpu
+from jax.sharding import Mesh
 from jax.sharding import PartitionSpec as P
 
 F32 = jnp.float32
 BF16 = jnp.bfloat16
 VMEM_LIMIT = 24 * 1024 * 1024
+
+
+BA = ("xl", "y", "core")
+COL = ("xh", "z")
+
+
+def place():
+    i = (lax.axis_index("xl") * 4 + lax.axis_index("y")) * 2 + lax.axis_index("core")
+    return i, lax.axis_index("xh") * 4 + lax.axis_index("z")
 
 
 def lane_bits(g):
@@ -51,48 +61,72 @@
 
 def cube_kernel(r_ref, w_ref, out_ref, x_ref):
     step = pl.program_id(0)
-    base = lax.axis_index("ba") ^ (2 * lax.axis_index("col"))
+    i, j = place()
+    base = i ^ (2 * j)
     top = lax.broadcasted_iota(jnp.int32, (8, 128), 0) < 4
     masks = lane_bits(0)
-    for half in range(2):
-        acc = None
-        for m in range(3):
-            rows = w_ref[m, :, 32 * half : 32 * half + 32, :].reshape(256, 512)
-            term = lax.dot_general(
-                r_ref[m], rows, (((1,), (1,)), ((), ())), preferred_element_type=F32
-            )
-            acc = term if acc is None else acc + term
-        x_ref[half] = acc.reshape(16, 32, 256)
-
-    @pl.loop(0, 16)
-    def _(a_hi):
-        h = a_hi ^ base
-        for tile in range(2):
-            lanes = slice(128 * tile, 128 * tile + 128)
-            values = []
-            for t in range(4):
-                values += halves(
-                    x_ref[0, a_hi, 8 * t : 8 * t + 8, lanes],
-                    x_ref[1, a_hi ^ 1, 8 * t : 8 * t + 8, lanes],
-                    top,
+
+    def multiply():
+        for half in range(2):
+            acc = None
+            for m in range(3):
+                rows = w_ref[m, :, 32 * half : 32 * half + 32, :].reshape(256, 512)
+                term = lax.dot_general(
+                    r_ref[m], rows, (((1,), (1,)), ((), ())), preferred_element_type=F32
                 )
-            for k, value in enumerate(butterfly(values, masks)):
-                g = k ^ (2 * step + tile)
-                out_ref[8 * h + g, :, lanes] = value.astype(BF16)
+                acc = term if acc is None else acc + term
+            x_ref[step % 2, half] = acc.reshape(16, 32, 256)
+
+    def send():
+        old = (step + 1) % 2
+        for a_hi in range(16):
+            h = a_hi ^ base
+            for tile in range(2):
+                lanes = slice(128 * tile, 128 * tile + 128)
+                values = []
+                for t in range(4):
+                    values += halves(
+                        x_ref[old, 0, a_hi, 8 * t : 8 * t + 8, lanes],
+                        x_ref[old, 1, a_hi ^ 1, 8 * t : 8 * t + 8, lanes],
+                        top,
+                    )
+                for k, value in enumerate(butterfly(values, masks)):
+                    g = k ^ (2 * (step - 1) + tile)
+                    out_ref[8 * h + g, :, lanes] = value.astype(BF16)
+
+    in_turn(step, multiply, send)
+
+
+def in_turn(step, first, second):
+    @pl.when(step == 0)
+    def _():
+        first()
+
+    @pl.when((step > 0) & (step < 4))
+    def _():
+        second()
+        first()
+
+    @pl.when(step == 4)
+    def _():
+        second()
 
 
 def make_cubes(r_pairs, w):
     return pl.pallas_call(
         cube_kernel,
-        grid=(4,),
+        grid=(5,),
         in_specs=[
             whole((3, 512, 512)),
-            pl.BlockSpec((3, 8, 64, 512), lambda s: (0, s, 0, 0)),
+            pl.BlockSpec((3, 8, 64, 512), lambda s: (0, jnp.minimum(s, 3), 0, 0)),
         ],
-        out_specs=pl.BlockSpec((128, 8, 256), lambda s: (0, 0, s)),
+        out_specs=pl.BlockSpec((128, 8, 256), lambda s: (0, 0, jnp.maximum(s - 1, 0))),
         out_shape=jax.ShapeDtypeStruct((128, 8, 1024), BF16),
-        scratch_shapes=[pltpu.VMEM((2, 16, 32, 256), F32)],
+        scratch_shapes=[pltpu.VMEM((2, 2, 16, 32, 256), F32)],
         compiler_params=params(58 * 1024 * 1024),
+        cost_estimate=pl.CostEstimate(
+            flops=2 * 512 * 2048 * 1536, bytes_accessed=10 * 1024**2, transcendentals=0
+        ),
         name="cubes",
     )(r_pairs, w)
 
@@ -107,7 +141,7 @@
     energy_ref, ec_ref, m_ref, perm_ref, turn_ref, out_ref,
     mf_ref, mp_ref, part_ref, table_ref, eb_ref, s_ref, turned_ref, q_ref, comb_ref,
 ):
-    h, g = lax.axis_index("ba"), lax.axis_index("col")
+    h, g = place()
     lane = lax.broadcasted_iota(jnp.int32, (8, 128), 1)
     lanes = lane_bits(g)
     rows = [owner_bits(h, c_h) for c_h in range(2)]
@@ -188,7 +222,7 @@
                     for i in range(16):
                         total = s_ref[x, i, a_r, 8 * c_h : 8 * c_h + 8, :].astype(F32) + values[i]
                         den = (table_ref[x, i ^ c_h, a_r] - eb_ref[x, i : i + 1]) - ec_ref[c_h]
-                        comb_ref[x, i, pl.ds(9 * (4 * c_h + a_r), 8), :] = total / den
+                        comb_ref[x, i ^ c_h ^ (h & 1), pl.ds(9 * (4 * c_h + a_r), 8), :] = total / den
 
     @pl.loop(0, 16)
     def _(i):
@@ -228,50 +262,52 @@
     )(energy, ec, m, jnp.asarray(perm, BF16), jnp.asarray(turn, BF16))
 
 
-def contract_kernel(m_ref, w_ref, out_ref, comb_ref, sum_ref):
+def contract_kernel(m_ref, w_ref, other_ref, out_ref, comb_ref, sum_ref):
     step = pl.program_id(0)
-    base = lax.axis_index("ba") ^ (2 * lax.axis_index("col"))
+    i, j = place()
+    base = (i >> 1) ^ j
     top = lax.broadcasted_iota(jnp.int32, (8, 128), 0) < 4
     masks = lane_bits(0)
 
-    @pl.loop(0, 16)
-    def _(a_hi):
-        h = a_hi ^ base
-        for tile in range(2):
-            lanes = slice(128 * tile, 128 * tile + 128)
-            values = []
-            for k in range(8):
-                g = k ^ (2 * step + tile)
-                values.append(m_ref[8 * h + g, :, lanes].astype(F32))
-            values = butterfly(values, masks)
-            for t in range(2):
-                first = halves(values[4 * t], values[4 * t + 1], top)
-                second = halves(values[4 * t + 2], values[4 * t + 3], top)
-                for half in range(2):
-                    rows = jnp.concatenate([first[half], second[half]], axis=0).astype(BF16)
-                    comb_ref[half, a_hi ^ half, 16 * t : 16 * t + 16, lanes] = rows
-
-    for m in range(3):
-        term = None
-        for half in range(2):
-            rows = w_ref[m, :, 32 * half : 32 * half + 32, :].reshape(256, 512)
-            left = comb_ref[half].reshape(512, 256)
-            product = jnp.dot(left, rows, preferred_element_type=F32)
-            term = product if term is None else term + product
-
-        @pl.when(step == 0)
-        def _(m=m, term=term):
-            sum_ref[m] = term
-
-        @pl.when(step > 0)
-        def _(m=m, term=term):
-            sum_ref[m] = sum_ref[m] + term
-
-    @pl.when(step == 3)
+    def receive():
+        for block in range(8):
+            for low in range(2):
+                h = 2 * (block ^ base) + low
+                for tile in range(2):
+                    lanes = slice(128 * tile, 128 * tile + 128)
+                    values = []
+                    for k in range(8):
+                        g = k ^ (2 * step + tile)
+                        values.append(m_ref[8 * h + g, :, lanes].astype(F32))
+                    values = butterfly(values, masks)
+                    for t in range(2):
+                        first = halves(values[4 * t], values[4 * t + 1], top)
+                        second = halves(values[4 * t + 2], values[4 * t + 3], top)
+                        for half in range(2):
+                            start = 512 * (low ^ half) + 256 * half + 128 * tile
+                            rows = jnp.concatenate([first[half], second[half]], axis=0)
+                            row = 32 * block + 16 * t
+                            comb_ref[step % 2, row : row + 16, start : start + 128] = rows.astype(BF16)
+
+    def multiply():
+        for m in range(3):
+            rows = [
+                ref[m, :, 32 * half : 32 * half + 32, :].reshape(256, 512)
+                for ref in (w_ref, other_ref)
+                for half in range(2)
+            ]
+            term = jnp.dot(
+                comb_ref[(step + 1) % 2], jnp.concatenate(rows, axis=0), preferred_element_type=F32
+            )
+            sum_ref[m] = term + jnp.where(step > 1, sum_ref[m], 0.0)
+
+    in_turn(step, receive, multiply)
+
+    @pl.when(step == 4)
     def _():
         low = lax.broadcasted_iota(jnp.int32, (16, 128), 1) < 64
         for m in range(3):
-            for k in range(16):
+            for k in range(8):
                 for t in range(4):
                     column = slice(128 * t, 128 * t + 128)
                     upper = sum_ref[m, 32 * k : 32 * k + 16, column]
@@ -282,25 +318,27 @@
                     out_ref[k, 2 * t + 1, 16 * m : 16 * m + 16, :] = odd.astype(BF16)
 
 
-def contract(m, w):
+def contract(m, w, other):
+    behind = pl.BlockSpec((3, 8, 64, 512), lambda s: (0, jnp.maximum(s - 1, 0), 0, 0))
     return pl.pallas_call(
         contract_kernel,
-        grid=(4,),
+        grid=(5,),
         in_specs=[
-            pl.BlockSpec((128, 8, 256), lambda s: (0, 0, s)),
-            pl.BlockSpec((3, 8, 64, 512), lambda s: (0, s, 0, 0)),
+            pl.BlockSpec((128, 8, 256), lambda s: (0, 0, jnp.minimum(s, 3))),
+            behind,
+            behind,
         ],
-        out_specs=whole((16, 8, 48, 128)),
-        out_shape=jax.ShapeDtypeStruct((16, 8, 48, 128), BF16),
-        scratch_shapes=[pltpu.VMEM((2, 16, 32, 256), BF16), pltpu.VMEM((3, 512, 512), F32)],
+        out_specs=whole((8, 8, 48, 128)),
+        out_shape=jax.ShapeDtypeStruct((8, 8, 48, 128), BF16),
+        scratch_shapes=[pltpu.VMEM((2, 256, 1024), BF16), pltpu.VMEM((3, 256, 512), F32)],
         compiler_params=params(),
         name="contract",
-    )(m, w)
+    )(m, w, other)
 
 
 def total_kernel(parts_ref, out_ref):
     total = parts_ref[0:8].astype(F32).sum(axis=0)
-    for s in range(1, 16):
+    for s in range(1, 8):
         total = total + parts_ref[8 * s : 8 * s + 8].astype(F32).sum(axis=0)
     for m in range(3):
         out_ref[m, 0:16, :] = total[16 * m : 16 * m + 16, 0:64]
@@ -322,20 +360,21 @@
 
 def on_device(r_pairs, w_tiles, virt_energy, energy_shift):
     w = w_tiles[0]
+    other = lax.ppermute(w, "core", [(0, 1), (1, 0)])
     ec = jnp.broadcast_to(virt_energy.reshape(8, 2, 1, 32), (8, 2, 4, 32))
     ec = jnp.swapaxes(ec.reshape(8, 2, 128), 0, 1)
     energy = jnp.concatenate([virt_energy, jnp.broadcast_to(energy_shift, (128,))])
     cubes, ec, energy = lax.optimization_barrier((make_cubes(r_pairs[0], w), ec, energy))
-    met = exchange(cubes, ("ba", "col"))
-    combined = combine_at_owner(energy, ec, met)
-    home = exchange(combined, ("ba", "col"))
-    arrived = exchange(contract(home, w).reshape(128, 48, 128), ("ba", "col"))
-    return total_of(arrived)[None]
+    met = exchange(cubes, BA + COL)
+    home = exchange(combine_at_owner(energy, ec, met), BA + COL)
+    parts = contract(home, w, other).reshape(64, 48, 128)
+    return total_of(exchange(parts, ("xl", "y") + COL))[None]
 
 
 def solution(mesh):
-    in_specs = (P(), P(None, None, "ba", "col", None), P(), P())
-    out_specs = P(None, None, "ba", "col")
+    mesh = Mesh(mesh.devices.reshape(2, 4, 2, 2, 4), BA + COL)
+    in_specs = (P(), P(None, None, BA, COL, None), P(), P())
+    out_specs = P(None, None, BA, COL)
     return jax.shard_map(
         on_device, mesh=mesh, in_specs=in_specs, out_specs=out_specs, check_vma=False
     )

time: 134 us -> 125 us (0.933)
  blocking collectives: 103 us -> 95.5 us
  Pallas kernels: 28.9 us -> 26.9 us
    all_to_all x3, blocking collectives: 103 us -> 95.5 us  [exchange(): return lax.all_to_all(x, axis, split_axis=0, concat_axis=0, tiled=True)]
    pallas_call x2, Pallas kernels: 17.9 us -> 16 us  [the longest x1 8.64 us: make_cubes(): pl.pallas_call(cube_kernel, grid=(5,), in_specs=[whole((3, 512, 512)), pl...]
  transfers between devices with their start and end apart: 0 -> 1, of which waited for: 0 -> 0; matrix products, arithmetic and copies ran while one was open for 0% -> 1% of each run, Pallas kernels for 0% -> 15%
where the time goes in v5:
time: 125 us
  blocking collectives  95.5 us (76%)
  Pallas kernels  26.9 us (22%)
  local copies, waits for them, and re-layouts  1.56 us (1%)
    all_to_all x3, blocking collectives, exchange(): return lax.all_to_all(x, axis, split_axis=0, concat_axis=0, tiled=True)  95.5 us
    pallas_call x1, Pallas kernels, combine_at_owner(): pl.pallas_call(owner_kernel, in_specs=[SMEM_SPEC, VMEM_SPEC, VMEM_SPEC, V...  10.1 us
    pallas_call x1, Pallas kernels, make_cubes(): pl.pallas_call(cube_kernel, grid=(5,), in_specs=[whole((3, 512, 512)), pl...  8.64 us
    pallas_call x1, Pallas kernels, contract(): pl.pallas_call(contract_kernel, grid=(5,), in_specs=[pl.BlockSpec((128, 8...  7.36 us
  transfers between devices with their start and end apart: 1, of which 0 were waited for; matrix products, arithmetic and copies ran while one was open for 1% of the time, Pallas kernels for 15%

profile of v5, /device:TPU:0, one launch (start us, length us, event | category | flops | bytes accessed | tf_op | source)
XLA Modules:
  0.0 124.6 jit_solution(5762951076399087282)
XLA Ops:
  0.0 0.0 collective-permute-start
  0.7 0.8 broadcast_in_dim.15
  1.4 0.7 concatenate.3.energy_ref
  2.1 0.1 reshape.8
  2.2 0.0 copy-start
  2.2 0.0 copy-start.1
  2.2 8.6 %cubes.1 = bf16[128,8,1024]{2,1,0:T(8,128)(2,1)} custom-call(bf16[3,512,512]{2,1,0:T(8,128)(2,1)} %bitcast.16, bf16[3,32,64,512]{3,2,1,0:T(8,128)(2,1)} %bitcast.10), custom_call_target="tpu_custom_call" | custom-call | flops 3221225472 | bytes 10485760 | tf_op jit(solution)/shard_map/cubes/pallas_call | solution.py:116
  10.9 0.0 slice-start
  10.9 40.3 %all_to_all.15.m_ref = bf16[128,8,1024]{2,1,0:T(8,128)(2,1)S(1)} all-to-all(bf16[128,8,1024]{2,1,0:T(8,128)(2,1)} %cubes.1), channel_id=1, replica_groups=mesh['xl'=2,'y'=4,'core'=2,'xh'=2,'z'=4] {'xl','y','core','xh','z'}, dimensions={0} | all-to-all | bytes 4194304 | tf_op jit(solution)/shard_map/all_to_all | solution.py:358
  51.1 0.0 copy-done
  51.1 0.0 copy-done.1
  51.1 0.0 slice-start.1
  51.1 10.1 %combine_at_owner.1 = bf16[128,8,1024]{2,1,0:T(8,128)(2,1)S(1)} custom-call(f32[640]{0:T(1024)S(1)} %concatenate.3.energy_ref, f32[2,8,128]{2,1,0:T(8,128)S(1)} %bitcast.15, bf16[128,8,1024]{2,1,0:T(8,128)(2,1)S(1)} %all_to_all.15.m_ref, bf16[1024,1024]{1,0:T(8,128)(2,1)S(1)} %copy-done, bf16[512,512]{1,0:T(8,128)(2,1)S(1)} %copy-done.1), custom_call_target="tpu_custom_call" | custom-call | tf_op jit(solution)/shard_map/combine_at_owner/pallas_call | solution.py:244
  61.2 34.2 %all_to_all.16.m_ref = bf16[128,8,1024]{2,1,0:T(8,128)(2,1)S(1)} all-to-all(bf16[128,8,1024]{2,1,0:T(8,128)(2,1)S(1)} %combine_at_owner.1), channel_id=1, replica_groups=mesh['xl'=2,'y'=4,'core'=2,'xh'=2,'z'=4] {'xl','y','core','xh','z'}, dimensions={0} | all-to-all | bytes 4194304 | tf_op jit(solution)/shard_map/all_to_all | solution.py:358
  95.4 0.0 collective-permute-done.other_ref
  95.4 0.0 slice-done
  95.4 0.0 slice-done.1
  95.4 7.4 %contract.1 = bf16[8,8,48,128]{3,2,1,0:T(8,128)(2,1)S(1)} custom-call(bf16[128,8,1024]{2,1,0:T(8,128)(2,1)S(1)} %all_to_all.16.m_ref, bf16[3,32,64,512]{3,2,1,0:T(8,128)(2,1)S(1)} %bitcast.13, bf16[3,32,64,512]{3,2,1,0:T(8,128)(2,1)} %collective-permute-done.other_ref), custom_call_target="tpu_custom_call" | custom-call | tf_op jit(solution)/shard_map/contract/pallas_call | solution.py:323
  102.8 21.0 %all_to_all.17.parts_ref = bf16[64,48,128]{2,1,0:T(8,128)(2,1)S(1)} all-to-all(bf16[64,48,128]{2,1,0:T(8,128)(2,1)S(1)} %bitcast.14), channel_id=1, replica_groups=mesh['xl'=2,'y'=4,'core'=2,'xh'=2,'z'=4] {'xl','y','xh','z'}, dimensions={0} | all-to-all | bytes 1572864 | tf_op jit(solution)/shard_map/all_to_all | solution.py:358
  123.8 0.8 total.1
  (3 shorter events, 0.0 us)
Async XLA Ops:
  0.0 95.4 %collective-permute-start = (bf16[3,32,64,512]{3,2,1,0:T(8,128)(2,1)}, bf16[3,32,64,512]{3,2,1,0:T(8,128)(2,1)}, u32[]{:S(2)}, u32[]{:S(2)}) collective-permute-start(bf16[3,32,64,512]{3,2,1,0:T(8,128)(2,1)} %bitcast.9), channel_id=1, source_target_pairs={{0,8},{8,0},{1,9},{9,1},{2,10},{10,2},{3,11},{11,3},{4,12},{12,4},... | collective-permute-start | bytes 18874376 | tf_op jit(solution)/shard_map/ppermute | solution.py:363
  2.2 48.9 %copy-start = (bf16[1024,1024]{1,0:T(8,128)(2,1)S(1)}, bf16[1024,1024]{1,0:T(8,128)(2,1)}, u32[]{:S(2)}) copy-start(bf16[1024,1024]{1,0:T(8,128)(2,1)} %constant.4.clone.perm_ref) | copy-start | bytes 6291460
  2.2 48.9 %copy-start.1 = (bf16[512,512]{1,0:T(8,128)(2,1)S(1)}, bf16[512,512]{1,0:T(8,128)(2,1)}, u32[]{:S(2)}) copy-start(bf16[512,512]{1,0:T(8,128)(2,1)} %constant.5.clone.turn_ref) | copy-start | bytes 1572868
  10.9 84.5 %slice-start = ((s8[6291456]{0:T(1024)(128)(4,1)}), s8[4194304]{0:T(1024)(128)(4,1)S(1)}, s32[]{:S(2)}) async-start(s8[6291456]{0:T(1024)(128)(4,1)} %bitcast.11), calls=%async_computation.3 | async-start | bytes 8388608
  51.1 44.3 %slice-start.1 = ((s8[6291456]{0:T(1024)(128)(4,1)}), s8[2097152]{0:T(1024)(128)(4,1)S(1)}, s32[]{:S(2)}) async-start(s8[6291456]{0:T(1024)(128)(4,1)} %bitcast.11), calls=%async_computation.4 | async-start | bytes 4194304

commit v6 on v5

--- a/solution.py
+++ b/solution.py
@@ -59,7 +59,7 @@
 SMEM_SPEC = pl.BlockSpec(memory_space=pltpu.SMEM)
 
 
-def cube_kernel(r_ref, w_ref, out_ref, x_ref):
+def cube_kernel(r_ref, w_ref, _, out_ref, x_ref):
     step = pl.program_id(0)
     i, j = place()
     base = i ^ (2 * j)
@@ -112,13 +112,14 @@
         second()
 
 
-def make_cubes(r_pairs, w):
+def make_cubes(r_pairs, w, shift):
     return pl.pallas_call(
         cube_kernel,
         grid=(5,),
         in_specs=[
             whole((3, 512, 512)),
             pl.BlockSpec((3, 8, 64, 512), lambda s: (0, jnp.minimum(s, 3), 0, 0)),
+            whole((1, 1)),
         ],
         out_specs=pl.BlockSpec((128, 8, 256), lambda s: (0, 0, jnp.maximum(s - 1, 0))),
         out_shape=jax.ShapeDtypeStruct((128, 8, 1024), BF16),
@@ -128,7 +129,7 @@
             flops=2 * 512 * 2048 * 1536, bytes_accessed=10 * 1024**2, transcendentals=0
         ),
         name="cubes",
-    )(r_pairs, w)
+    )(r_pairs, w, shift)
 
 
 def owner_bits(h, c_h):
@@ -138,44 +139,54 @@
 
 
 def owner_kernel(
-    energy_ref, ec_ref, m_ref, perm_ref, turn_ref, out_ref,
-    mf_ref, mp_ref, part_ref, table_ref, eb_ref, s_ref, turned_ref, q_ref, comb_ref,
+    energy_ref, rows_ref, shift_ref, m_ref, perm_ref, turn_ref, out_ref,
+    ec_ref, mf_ref, mp_ref, part_ref, table_ref, eb_ref, s_ref, turned_ref, q0_ref, q1_ref, comb_ref,
 ):
     h, g = place()
     lane = lax.broadcasted_iota(jnp.int32, (8, 128), 1)
     lanes = lane_bits(g)
     rows = [owner_bits(h, c_h) for c_h in range(2)]
-    shift = energy_ref[512]
-
-    @pl.loop(0, 4)
+    shift = jnp.broadcast_to(shift_ref[...], (8, 128))
+
+    twice = jnp.concatenate([rows_ref[...], rows_ref[...]], axis=0)
+    for source in range(4):
+        spread = twice
+        for step in range(1, 4):
+            there = lane // 32 == (source + step) % 4
+            spread = jnp.where(there, pltpu.roll(twice, 32 * step, 1), spread)
+        for row in range(4):
+            j = 2 * row + source // 2
+            ec_ref[source % 2, j : j + 1] = spread[row : row + 1]
+
+    @pl.loop(0, 2)
     def _(part):
-        columns = pl.ds(pl.multiple_of(256 * part, 256), 256)
+        columns = pl.ds(pl.multiple_of(512 * part, 512), 512)
         moved = jnp.dot(
             m_ref[...].reshape(1024, 1024), perm_ref[:, columns], preferred_element_type=F32
         )
-        for odd in range(2):
-            x = 2 * part + odd
+        for tile in range(4):
+            x = 4 * part + tile
             for j in range(8):
                 for i in range(16):
                     row = 8 * (8 * i + j)
                     mp_ref[x, pl.ds(129 * (row // 128) + row % 128, 8), :] = moved[
-                        row : row + 8, 128 * odd : 128 * odd + 128
+                        row : row + 8, 128 * tile : 128 * tile + 128
                     ]
-                    column = pl.ds(pl.multiple_of(256 * part + 128 * odd, 128), 128)
+                    column = pl.ds(pl.multiple_of(512 * part + 128 * tile, 128), 128)
                     mf_ref[x, i, 9 * j : 9 * j + 8, :] = m_ref[8 * i + j, :, column].astype(F32)
         for a_r in range(4):
-            for odd in range(2):
-                x = 2 * part + odd
+            for tile in range(4):
+                x = 4 * part + tile
                 values = [
-                    jnp.full((8, 128), shift - energy_ref[32 * i + 4 * x + a_r], F32)
+                    shift - energy_ref[i // 4, 32 * (i % 4) + 4 * x + a_r]
                     for i in range(16)
                 ]
                 for i, value in enumerate(butterfly(values, rows[0])):
                     part_ref[x, i, a_r] = value
-        for odd in range(2):
-            x = 2 * part + odd
+        for tile in range(4):
+            x = 4 * part + tile
             for i in range(16):
-                b = [jnp.full((1, 128), energy_ref[32 * i + 4 * x + r], F32) for r in range(4)]
+                b = [jnp.full((1, 128), energy_ref[i // 4, 32 * (i % 4) + 4 * x + r], F32) for r in range(4)]
                 low = jnp.where(lane[0:1] < 32, b[0], b[1])
                 high = jnp.where(lane[0:1] < 96, b[2], b[3])
                 eb_ref[x, i : i + 1] = jnp.where(lane[0:1] < 64, low, high)
@@ -202,27 +213,31 @@
                 for x in range(8):
                     table_ref[x, i, a_r] = values[x]
 
-    for half in range(2):
+    def turn(x, q_ref):
         q_ref[...] = jnp.dot(
-            turned_ref[...].reshape(2048, 512),
-            turn_ref[:, 256 * half : 256 * half + 256],
-            preferred_element_type=F32,
-        ).reshape(8, 16, 16, 256)
-
-        @pl.loop(0, 8)
-        def _(x, half=half):
-            for odd in range(2):
-                a_r = 2 * half + odd
-                for c_h in range(2):
-                    values = [
-                        q_ref[x, i, 8 * c_h : 8 * c_h + 8, 128 * odd : 128 * odd + 128]
-                        for i in range(16)
-                    ]
-                    values = butterfly(values, rows[c_h])
-                    for i in range(16):
-                        total = s_ref[x, i, a_r, 8 * c_h : 8 * c_h + 8, :].astype(F32) + values[i]
-                        den = (table_ref[x, i ^ c_h, a_r] - eb_ref[x, i : i + 1]) - ec_ref[c_h]
-                        comb_ref[x, i ^ c_h ^ (h & 1), pl.ds(9 * (4 * c_h + a_r), 8), :] = total / den
+            turned_ref[x].reshape(256, 512), turn_ref[...], preferred_element_type=F32
+        ).reshape(16, 16, 512)
+
+    def divide(x, q_ref):
+        for a_r in range(4):
+            for c_h in range(2):
+                values = [
+                    q_ref[i, 8 * c_h : 8 * c_h + 8, 128 * a_r : 128 * a_r + 128] for i in range(16)
+                ]
+                values = butterfly(values, rows[c_h])
+                for i in range(16):
+                    total = s_ref[x, i, a_r, 8 * c_h : 8 * c_h + 8, :].astype(F32) + values[i]
+                    den = (table_ref[x, i ^ c_h, a_r] - eb_ref[x, i : i + 1]) - ec_ref[c_h]
+                    comb_ref[x, i ^ c_h ^ (h & 1), pl.ds(9 * (4 * c_h + a_r), 8), :] = total / den
+
+    turn(0, q0_ref)
+
+    @pl.loop(0, 4)
+    def _(pair):
+        turn(2 * pair + 1, q1_ref)
+        divide(2 * pair, q0_ref)
+        turn(jnp.minimum(2 * pair + 2, 7), q0_ref)
+        divide(2 * pair + 1, q1_ref)
 
     @pl.loop(0, 16)
     def _(i):
@@ -235,7 +250,7 @@
 VMEM_SPEC = pl.BlockSpec(memory_space=pltpu.VMEM)
 
 
-def combine_at_owner(energy, ec, m):
+def combine_at_owner(energy, shift, m):
     source = np.arange(1024)
     perm = ((source % 32) * 32 + source // 32)[:, None] == source[None, :]
     source = np.arange(512)
@@ -243,10 +258,11 @@
     turn = turned[:, None] == source[None, :]
     return pl.pallas_call(
         owner_kernel,
-        in_specs=[SMEM_SPEC, VMEM_SPEC, VMEM_SPEC, VMEM_SPEC, VMEM_SPEC],
+        in_specs=[SMEM_SPEC] + [VMEM_SPEC] * 5,
         out_specs=VMEM_SPEC,
         out_shape=jax.ShapeDtypeStruct((128, 8, 1024), BF16),
         scratch_shapes=[
+            pltpu.VMEM((2, 8, 128), F32),
             pltpu.VMEM((8, 16, 72, 128), F32),
             pltpu.VMEM((8, 1032, 128), F32),
             pltpu.VMEM((8, 16, 4, 8, 128), F32),
@@ -254,12 +270,13 @@
             pltpu.VMEM((8, 16, 128), F32),
             pltpu.VMEM((8, 16, 4, 16, 128), BF16),
             pltpu.VMEM((8, 16, 16, 512), BF16),
-            pltpu.VMEM((8, 16, 16, 256), F32),
+            pltpu.VMEM((16, 16, 512), F32),
+            pltpu.VMEM((16, 16, 512), F32),
             pltpu.VMEM((8, 16, 72, 128), F32),
         ],
         compiler_params=params(40 * 1024 * 1024),
         name="combine_at_owner",
-    )(energy, ec, m, jnp.asarray(perm, BF16), jnp.asarray(turn, BF16))
+    )(energy, energy, shift, m, jnp.asarray(perm, BF16), jnp.asarray(turn, BF16))
 
 
 def contract_kernel(m_ref, w_ref, other_ref, out_ref, comb_ref, sum_ref):
@@ -360,13 +377,11 @@
 
 def on_device(r_pairs, w_tiles, virt_energy, energy_shift):
     w = w_tiles[0]
-    other = lax.ppermute(w, "core", [(0, 1), (1, 0)])
-    ec = jnp.broadcast_to(virt_energy.reshape(8, 2, 1, 32), (8, 2, 4, 32))
-    ec = jnp.swapaxes(ec.reshape(8, 2, 128), 0, 1)
-    energy = jnp.concatenate([virt_energy, jnp.broadcast_to(energy_shift, (128,))])
-    cubes, ec, energy = lax.optimization_barrier((make_cubes(r_pairs[0], w), ec, energy))
+    energy, shift = virt_energy.reshape(4, 128), energy_shift.reshape(1, 1)
+    cubes, later = lax.optimization_barrier((make_cubes(r_pairs[0], w, shift), w))
+    other = lax.ppermute(later, "core", [(0, 1), (1, 0)])
     met = exchange(cubes, BA + COL)
-    home = exchange(combine_at_owner(energy, ec, met), BA + COL)
+    home = exchange(combine_at_owner(energy, shift, met), BA + COL)
     parts = contract(home, w, other).reshape(64, 48, 128)
     return total_of(exchange(parts, ("xl", "y") + COL))[None]
 

time: 125 us -> 122 us (0.976)
  Pallas kernels: 26.9 us -> 25 us
  local copies, waits for them, and re-layouts: 1.56 us -> 0.02 us
  transfers between devices with their start and end apart: 1 -> 1, of which waited for: 0 -> 0; matrix products, arithmetic and copies ran while one was open for 1% -> 0% of each run, Pallas kernels for 15% -> 8%
where the time goes in v6:
time: 122 us; the launch traced here: 121 us
  blocking collectives  95.5 us (78%)
  Pallas kernels  25 us (20%)
    all_to_all x3, blocking collectives, exchange(): return lax.all_to_all(x, axis, split_axis=0, concat_axis=0, tiled=True)  95.5 us
    pallas_call x1, Pallas kernels, combine_at_owner(): pl.pallas_call(owner_kernel, in_specs=[SMEM_SPEC] + [VMEM_SPEC] * 5, out_...  9.38 us
    pallas_call x1, Pallas kernels, make_cubes(): pl.pallas_call(cube_kernel, grid=(5,), in_specs=[whole((3, 512, 512)), pl...  8.51 us
    pallas_call x1, Pallas kernels, contract(): pl.pallas_call(contract_kernel, grid=(5,), in_specs=[pl.BlockSpec((128, 8...  6.32 us
  transfers between devices with their start and end apart: 1, of which 0 were waited for; matrix products, arithmetic and copies ran while one was open for 0% of the time, Pallas kernels for 8%

profile of v6, /device:TPU:0, one launch (start us, length us, event | category | flops | bytes accessed | tf_op | source)
XLA Modules:
  0.0 121.3 jit_solution(3900230491812063641)
XLA Ops:
  0.7 8.5 %cubes.1 = bf16[128,8,1024]{2,1,0:T(8,128)(2,1)} custom-call(bf16[3,512,512]{2,1,0:T(8,128)(2,1)} %bitcast.16, bf16[3,32,64,512]{3,2,1,0:T(8,128)(2,1)} %bitcast.8, f32[1,1]{1,0:T(1,128)} %bitcast.6._), custom_call_target="tpu_custom_call" | custom-call | flops 3221225472 | bytes 10485760 | tf_op jit(solution)/shard_map/cubes/pallas_call | solution.py:116
  9.2 0.0 copy-start
  9.2 0.0 copy-start.1
  9.2 0.0 copy-start.2
  9.2 0.1 collective-permute-start
  9.3 0.0 slice-start
  9.3 40.2 %all_to_all.15.m_ref = bf16[128,8,1024]{2,1,0:T(8,128)(2,1)S(1)} all-to-all(bf16[128,8,1024]{2,1,0:T(8,128)(2,1)} %cubes.1), channel_id=1, replica_groups=mesh['xl'=2,'y'=4,'core'=2,'xh'=2,'z'=4] {'xl','y','core','xh','z'}, dimensions={0} | all-to-all | bytes 4194304 | tf_op jit(solution)/shard_map/all_to_all | solution.py:375
  49.5 0.0 copy-done
  49.5 0.0 copy-done.1
  49.5 0.0 copy-done.2
  49.5 0.0 slice-start.1
  49.5 9.4 %combine_at_owner.1 = bf16[128,8,1024]{2,1,0:T(8,128)(2,1)S(1)} custom-call(f32[4,128]{1,0:T(4,128)S(1)} %bitcast.14, f32[4,128]{1,0:T(4,128)S(1)} %bitcast.15, f32[1,1]{1,0:T(1,128)} %bitcast.7.shift_ref, bf16[128,8,1024]{2,1,0:T(8,128)(2,1)S(1)} %all_to_all.15.m_ref, bf16[1024,1024]{1,0:T(8,128)(2,1)S(1)} %copy-done, bf16[512,512]{1,0:T(8,128)(2,1)S(1)} %copy-done.1), custom_call_target="tpu_custom_call" | custom-call | tf_op jit(solution)/shard_map/combine_at_owner/pallas_call | solution.py:259
  58.9 34.2 %all_to_all.16.m_ref = bf16[128,8,1024]{2,1,0:T(8,128)(2,1)S(1)} all-to-all(bf16[128,8,1024]{2,1,0:T(8,128)(2,1)S(1)} %combine_at_owner.1), channel_id=1, replica_groups=mesh['xl'=2,'y'=4,'core'=2,'xh'=2,'z'=4] {'xl','y','core','xh','z'}, dimensions={0} | all-to-all | bytes 4194304 | tf_op jit(solution)/shard_map/all_to_all | solution.py:375
  93.1 0.0 collective-permute-done.other_ref
  93.1 0.0 slice-done
  93.1 0.0 slice-done.1
  93.1 6.3 %contract.1 = bf16[8,8,48,128]{3,2,1,0:T(8,128)(2,1)S(1)} custom-call(bf16[128,8,1024]{2,1,0:T(8,128)(2,1)S(1)} %all_to_all.16.m_ref, bf16[3,32,64,512]{3,2,1,0:T(8,128)(2,1)S(1)} %bitcast.12, bf16[3,32,64,512]{3,2,1,0:T(8,128)(2,1)S(1)} %collective-permute-done.other_ref), custom_call_target="tpu_custom_call" | custom-call | tf_op jit(solution)/shard_map/contract/pallas_call | solution.py:340
  99.5 21.0 %all_to_all.17.parts_ref = bf16[64,48,128]{2,1,0:T(8,128)(2,1)S(1)} all-to-all(bf16[64,48,128]{2,1,0:T(8,128)(2,1)S(1)} %bitcast.13), channel_id=1, replica_groups=mesh['xl'=2,'y'=4,'core'=2,'xh'=2,'z'=4] {'xl','y','xh','z'}, dimensions={0} | all-to-all | bytes 1572864 | tf_op jit(solution)/shard_map/all_to_all | solution.py:375
  120.5 0.8 total.1
  (1 shorter events, 0.0 us)
Async XLA Ops:
  9.2 40.3 %copy-start = (bf16[1024,1024]{1,0:T(8,128)(2,1)S(1)}, bf16[1024,1024]{1,0:T(8,128)(2,1)}, u32[]{:S(2)}) copy-start(bf16[1024,1024]{1,0:T(8,128)(2,1)} %constant.4.clone.perm_ref) | copy-start | bytes 6291460
  9.2 40.3 %copy-start.1 = (bf16[512,512]{1,0:T(8,128)(2,1)S(1)}, bf16[512,512]{1,0:T(8,128)(2,1)}, u32[]{:S(2)}) copy-start(bf16[512,512]{1,0:T(8,128)(2,1)} %constant.5.clone.turn_ref) | copy-start | bytes 1572868
  9.2 40.3 %copy-start.2 = (f32[512]{0:T(512)S(1)}, f32[512]{0:T(512)}, u32[]{:S(2)}) copy-start(f32[512]{0:T(512)} %param.8) | copy-start | bytes 6148
  9.2 84.0 %collective-permute-start = (bf16[3,32,64,512]{3,2,1,0:T(8,128)(2,1)}, bf16[3,32,64,512]{3,2,1,0:T(8,128)(2,1)S(1)}, u32[]{:S(2)}, u32[]{:S(2)}) collective-permute-start(bf16[3,32,64,512]{3,2,1,0:T(8,128)(2,1)} %bitcast.9), channel_id=1, source_target_pairs={{0,8},{8,0},{1,9},{9,1},{2,10},{10,2},{3,11},{11,3},{4,12},{12,4},... | collective-permute-start | bytes 18874376 | tf_op jit(solution)/shard_map/ppermute | solution.py:382
  9.3 83.9 %slice-start = ((s8[6291456]{0:T(1024)(128)(4,1)}), s8[4194304]{0:T(1024)(128)(4,1)S(1)}, s32[]{:S(2)}) async-start(s8[6291456]{0:T(1024)(128)(4,1)} %bitcast.10), calls=%async_computation.3 | async-start | bytes 8388608
  49.5 43.6 %slice-start.1 = ((s8[6291456]{0:T(1024)(128)(4,1)}), s8[2097152]{0:T(1024)(128)(4,1)S(1)}, s32[]{:S(2)}) async-start(s8[6291456]{0:T(1024)(128)(4,1)} %bitcast.10), calls=%async_computation.4 | async-start | bytes 4194304

commit v7 on v6

--- a/solution.py
+++ b/solution.py
@@ -263,8 +263,8 @@
         out_shape=jax.ShapeDtypeStruct((128, 8, 1024), BF16),
         scratch_shapes=[
             pltpu.VMEM((2, 8, 128), F32),
-            pltpu.VMEM((8, 16, 72, 128), F32),
-            pltpu.VMEM((8, 1032, 128), F32),
+            pltpu.VMEM((8, 16, 80, 128), F32),
+            pltpu.VMEM((8, 1160, 128), F32),
             pltpu.VMEM((8, 16, 4, 8, 128), F32),
             pltpu.VMEM((8, 16, 4, 8, 128), F32),
             pltpu.VMEM((8, 16, 128), F32),
@@ -272,7 +272,7 @@
             pltpu.VMEM((8, 16, 16, 512), BF16),
             pltpu.VMEM((16, 16, 512), F32),
             pltpu.VMEM((16, 16, 512), F32),
-            pltpu.VMEM((8, 16, 72, 128), F32),
+            pltpu.VMEM((8, 16, 80, 128), F32),
         ],
         compiler_params=params(40 * 1024 * 1024),
         name="combine_at_owner",

time: 122 us -> 122 us (level)
  no operation moved by 1% of the time
where the time goes in v7:
time: 122 us; the launch traced here: 121 us
  blocking collectives  95.4 us (78%)
  Pallas kernels  25 us (20%)
    all_to_all x3, blocking collectives, exchange(): return lax.all_to_all(x, axis, split_axis=0, concat_axis=0, tiled=True)  95.4 us
    pallas_call x1, Pallas kernels, combine_at_owner(): pl.pallas_call(owner_kernel, in_specs=[SMEM_SPEC] + [VMEM_SPEC] * 5, out_...  9.4 us
    pallas_call x1, Pallas kernels, make_cubes(): pl.pallas_call(cube_kernel, grid=(5,), in_specs=[whole((3, 512, 512)), pl...  8.51 us
    pallas_call x1, Pallas kernels, contract(): pl.pallas_call(contract_kernel, grid=(5,), in_specs=[pl.BlockSpec((128, 8...  6.32 us
  transfers between devices with their start and end apart: 1, of which 0 were waited for; matrix products, arithmetic and copies ran while one was open for 0% of the time, Pallas kernels for 8%

profile of v7, /device:TPU:0, one launch (start us, length us, event | category | flops | bytes accessed | tf_op | source)
XLA Modules:
  0.0 121.3 jit_solution(11967659925211587417)
XLA Ops:
  0.7 8.5 %cubes.1 = bf16[128,8,1024]{2,1,0:T(8,128)(2,1)} custom-call(bf16[3,512,512]{2,1,0:T(8,128)(2,1)} %bitcast.16, bf16[3,32,64,512]{3,2,1,0:T(8,128)(2,1)} %bitcast.8, f32[1,1]{1,0:T(1,128)} %bitcast.6._), custom_call_target="tpu_custom_call" | custom-call | flops 3221225472 | bytes 10485760 | tf_op jit(solution)/shard_map/cubes/pallas_call | solution.py:116
  9.2 0.0 copy-start
  9.2 0.0 copy-start.1
  9.2 0.0 copy-start.2
  9.2 0.1 collective-permute-start
  9.3 0.0 slice-start
  9.3 40.2 %all_to_all.15.m_ref = bf16[128,8,1024]{2,1,0:T(8,128)(2,1)S(1)} all-to-all(bf16[128,8,1024]{2,1,0:T(8,128)(2,1)} %cubes.1), channel_id=1, replica_groups=mesh['xl'=2,'y'=4,'core'=2,'xh'=2,'z'=4] {'xl','y','core','xh','z'}, dimensions={0} | all-to-all | bytes 4194304 | tf_op jit(solution)/shard_map/all_to_all | solution.py:375
  49.5 0.0 copy-done
  49.5 0.0 copy-done.1
  49.5 0.0 copy-done.2
  49.5 0.0 slice-start.1
  49.5 9.4 %combine_at_owner.1 = bf16[128,8,1024]{2,1,0:T(8,128)(2,1)S(1)} custom-call(f32[4,128]{1,0:T(4,128)S(1)} %bitcast.14, f32[4,128]{1,0:T(4,128)S(1)} %bitcast.15, f32[1,1]{1,0:T(1,128)} %bitcast.7.shift_ref, bf16[128,8,1024]{2,1,0:T(8,128)(2,1)S(1)} %all_to_all.15.m_ref, bf16[1024,1024]{1,0:T(8,128)(2,1)S(1)} %copy-done, bf16[512,512]{1,0:T(8,128)(2,1)S(1)} %copy-done.1), custom_call_target="tpu_custom_call" | custom-call | tf_op jit(solution)/shard_map/combine_at_owner/pallas_call | solution.py:259
  58.9 34.2 %all_to_all.16.m_ref = bf16[128,8,1024]{2,1,0:T(8,128)(2,1)S(1)} all-to-all(bf16[128,8,1024]{2,1,0:T(8,128)(2,1)S(1)} %combine_at_owner.1), channel_id=1, replica_groups=mesh['xl'=2,'y'=4,'core'=2,'xh'=2,'z'=4] {'xl','y','core','xh','z'}, dimensions={0} | all-to-all | bytes 4194304 | tf_op jit(solution)/shard_map/all_to_all | solution.py:375
  93.1 0.0 collective-permute-done.other_ref
  93.1 0.0 slice-done
  93.1 0.0 slice-done.1
  93.2 6.3 %contract.1 = bf16[8,8,48,128]{3,2,1,0:T(8,128)(2,1)S(1)} custom-call(bf16[128,8,1024]{2,1,0:T(8,128)(2,1)S(1)} %all_to_all.16.m_ref, bf16[3,32,64,512]{3,2,1,0:T(8,128)(2,1)S(1)} %bitcast.12, bf16[3,32,64,512]{3,2,1,0:T(8,128)(2,1)S(1)} %collective-permute-done.other_ref), custom_call_target="tpu_custom_call" | custom-call | tf_op jit(solution)/shard_map/contract/pallas_call | solution.py:340
  99.5 21.0 %all_to_all.17.parts_ref = bf16[64,48,128]{2,1,0:T(8,128)(2,1)S(1)} all-to-all(bf16[64,48,128]{2,1,0:T(8,128)(2,1)S(1)} %bitcast.13), channel_id=1, replica_groups=mesh['xl'=2,'y'=4,'core'=2,'xh'=2,'z'=4] {'xl','y','xh','z'}, dimensions={0} | all-to-all | bytes 1572864 | tf_op jit(solution)/shard_map/all_to_all | solution.py:375
  120.5 0.8 total.1
  (1 shorter events, 0.0 us)
Async XLA Ops:
  9.2 40.3 %copy-start = (bf16[1024,1024]{1,0:T(8,128)(2,1)S(1)}, bf16[1024,1024]{1,0:T(8,128)(2,1)}, u32[]{:S(2)}) copy-start(bf16[1024,1024]{1,0:T(8,128)(2,1)} %constant.4.clone.perm_ref) | copy-start | bytes 6291460
  9.2 40.3 %copy-start.1 = (bf16[512,512]{1,0:T(8,128)(2,1)S(1)}, bf16[512,512]{1,0:T(8,128)(2,1)}, u32[]{:S(2)}) copy-start(bf16[512,512]{1,0:T(8,128)(2,1)} %constant.5.clone.turn_ref) | copy-start | bytes 1572868
  9.2 40.3 %copy-start.2 = (f32[512]{0:T(512)S(1)}, f32[512]{0:T(512)}, u32[]{:S(2)}) copy-start(f32[512]{0:T(512)} %param.8) | copy-start | bytes 6148
  9.2 84.0 %collective-permute-start = (bf16[3,32,64,512]{3,2,1,0:T(8,128)(2,1)}, bf16[3,32,64,512]{3,2,1,0:T(8,128)(2,1)S(1)}, u32[]{:S(2)}, u32[]{:S(2)}) collective-permute-start(bf16[3,32,64,512]{3,2,1,0:T(8,128)(2,1)} %bitcast.9), channel_id=1, source_target_pairs={{0,8},{8,0},{1,9},{9,1},{2,10},{10,2},{3,11},{11,3},{4,12},{12,4},... | collective-permute-start | bytes 18874376 | tf_op jit(solution)/shard_map/ppermute | solution.py:382
  9.3 83.9 %slice-start = ((s8[6291456]{0:T(1024)(128)(4,1)}), s8[4194304]{0:T(1024)(128)(4,1)S(1)}, s32[]{:S(2)}) async-start(s8[6291456]{0:T(1024)(128)(4,1)} %bitcast.10), calls=%async_computation.3 | async-start | bytes 8388608
  49.5 43.6 %slice-start.1 = ((s8[6291456]{0:T(1024)(128)(4,1)}), s8[2097152]{0:T(1024)(128)(4,1)S(1)}, s32[]{:S(2)}) async-start(s8[6291456]{0:T(1024)(128)(4,1)} %bitcast.10), calls=%async_computation.4 | async-start | bytes 4194304

commit v8 on v7

--- a/solution.py
+++ b/solution.py
@@ -172,8 +172,6 @@
                     mp_ref[x, pl.ds(129 * (row // 128) + row % 128, 8), :] = moved[
                         row : row + 8, 128 * tile : 128 * tile + 128
                     ]
-                    column = pl.ds(pl.multiple_of(512 * part + 128 * tile, 128), 128)
-                    mf_ref[x, i, 9 * j : 9 * j + 8, :] = m_ref[8 * i + j, :, column].astype(F32)
         for a_r in range(4):
             for tile in range(4):
                 x = 4 * part + tile
@@ -190,6 +188,13 @@
                 low = jnp.where(lane[0:1] < 32, b[0], b[1])
                 high = jnp.where(lane[0:1] < 96, b[2], b[3])
                 eb_ref[x, i : i + 1] = jnp.where(lane[0:1] < 64, low, high)
+
+    @pl.loop(0, 16)
+    def _(i):
+        for j in range(8):
+            for x in range(8):
+                block = m_ref[8 * i + j, :, 128 * x : 128 * x + 128]
+                mf_ref[x, i, 9 * j : 9 * j + 8, :] = block.astype(F32)
 
     @pl.loop(0, 8)
     def _(pair):

time: 122 us -> 121 us (level)
  no operation moved by 1% of the time
where the time goes in v8:
time: 121 us
  blocking collectives  95.4 us (79%)
  Pallas kernels  24.8 us (20%)
    all_to_all x3, blocking collectives, exchange(): return lax.all_to_all(x, axis, split_axis=0, concat_axis=0, tiled=True)  95.4 us
    pallas_call x1, Pallas kernels, combine_at_owner(): pl.pallas_call(owner_kernel, in_specs=[SMEM_SPEC] + [VMEM_SPEC] * 5, out_...  9.16 us
    pallas_call x1, Pallas kernels, make_cubes(): pl.pallas_call(cube_kernel, grid=(5,), in_specs=[whole((3, 512, 512)), pl...  8.51 us
    pallas_call x1, Pallas kernels, contract(): pl.pallas_call(contract_kernel, grid=(5,), in_specs=[pl.BlockSpec((128, 8...  6.32 us
  transfers between devices with their start and end apart: 1, of which 0 were waited for; matrix products, arithmetic and copies ran while one was open for 0% of the time, Pallas kernels for 8%

profile of v8, /device:TPU:0, one launch (start us, length us, event | category | flops | bytes accessed | tf_op | source)
XLA Modules:
  0.0 121.0 jit_solution(999595230634173722)
XLA Ops:
  0.7 8.5 %cubes.1 = bf16[128,8,1024]{2,1,0:T(8,128)(2,1)} custom-call(bf16[3,512,512]{2,1,0:T(8,128)(2,1)} %bitcast.16, bf16[3,32,64,512]{3,2,1,0:T(8,128)(2,1)} %bitcast.8, f32[1,1]{1,0:T(1,128)} %bitcast.6._), custom_call_target="tpu_custom_call" | custom-call | flops 3221225472 | bytes 10485760 | tf_op jit(solution)/shard_map/cubes/pallas_call | solution.py:116
  9.2 0.0 copy-start
  9.2 0.0 copy-start.1
  9.2 0.0 copy-start.2
  9.2 0.1 collective-permute-start
  9.3 0.0 slice-start
  9.3 40.2 %all_to_all.15.m_ref = bf16[128,8,1024]{2,1,0:T(8,128)(2,1)S(1)} all-to-all(bf16[128,8,1024]{2,1,0:T(8,128)(2,1)} %cubes.1), channel_id=1, replica_groups=mesh['xl'=2,'y'=4,'core'=2,'xh'=2,'z'=4] {'xl','y','core','xh','z'}, dimensions={0} | all-to-all | bytes 4194304 | tf_op jit(solution)/shard_map/all_to_all | solution.py:380
  49.5 0.0 copy-done
  49.5 0.0 copy-done.1
  49.5 0.0 copy-done.2
  49.5 0.0 slice-start.1
  49.5 9.2 %combine_at_owner.1 = bf16[128,8,1024]{2,1,0:T(8,128)(2,1)S(1)} custom-call(f32[4,128]{1,0:T(4,128)S(1)} %bitcast.14, f32[4,128]{1,0:T(4,128)S(1)} %bitcast.15, f32[1,1]{1,0:T(1,128)} %bitcast.7.shift_ref, bf16[128,8,1024]{2,1,0:T(8,128)(2,1)S(1)} %all_to_all.15.m_ref, bf16[1024,1024]{1,0:T(8,128)(2,1)S(1)} %copy-done, bf16[512,512]{1,0:T(8,128)(2,1)S(1)} %copy-done.1), custom_call_target="tpu_custom_call" | custom-call | tf_op jit(solution)/shard_map/combine_at_owner/pallas_call | solution.py:264
  58.7 34.2 %all_to_all.16.m_ref = bf16[128,8,1024]{2,1,0:T(8,128)(2,1)S(1)} all-to-all(bf16[128,8,1024]{2,1,0:T(8,128)(2,1)S(1)} %combine_at_owner.1), channel_id=1, replica_groups=mesh['xl'=2,'y'=4,'core'=2,'xh'=2,'z'=4] {'xl','y','core','xh','z'}, dimensions={0} | all-to-all | bytes 4194304 | tf_op jit(solution)/shard_map/all_to_all | solution.py:380
  92.9 0.0 collective-permute-done.other_ref
  92.9 0.0 slice-done
  92.9 0.0 slice-done.1
  92.9 6.3 %contract.1 = bf16[8,8,48,128]{3,2,1,0:T(8,128)(2,1)S(1)} custom-call(bf16[128,8,1024]{2,1,0:T(8,128)(2,1)S(1)} %all_to_all.16.m_ref, bf16[3,32,64,512]{3,2,1,0:T(8,128)(2,1)S(1)} %bitcast.12, bf16[3,32,64,512]{3,2,1,0:T(8,128)(2,1)S(1)} %collective-permute-done.other_ref), custom_call_target="tpu_custom_call" | custom-call | tf_op jit(solution)/shard_map/contract/pallas_call | solution.py:345
  99.2 21.0 %all_to_all.17.parts_ref = bf16[64,48,128]{2,1,0:T(8,128)(2,1)S(1)} all-to-all(bf16[64,48,128]{2,1,0:T(8,128)(2,1)S(1)} %bitcast.13), channel_id=1, replica_groups=mesh['xl'=2,'y'=4,'core'=2,'xh'=2,'z'=4] {'xl','y','xh','z'}, dimensions={0} | all-to-all | bytes 1572864 | tf_op jit(solution)/shard_map/all_to_all | solution.py:380
  120.2 0.8 total.1
  (1 shorter events, 0.0 us)
Async XLA Ops:
  9.2 40.3 %copy-start = (bf16[1024,1024]{1,0:T(8,128)(2,1)S(1)}, bf16[1024,1024]{1,0:T(8,128)(2,1)}, u32[]{:S(2)}) copy-start(bf16[1024,1024]{1,0:T(8,128)(2,1)} %constant.4.clone.perm_ref) | copy-start | bytes 6291460
  9.2 40.3 %copy-start.1 = (bf16[512,512]{1,0:T(8,128)(2,1)S(1)}, bf16[512,512]{1,0:T(8,128)(2,1)}, u32[]{:S(2)}) copy-start(bf16[512,512]{1,0:T(8,128)(2,1)} %constant.5.clone.turn_ref) | copy-start | bytes 1572868
  9.2 40.3 %copy-start.2 = (f32[512]{0:T(512)S(1)}, f32[512]{0:T(512)}, u32[]{:S(2)}) copy-start(f32[512]{0:T(512)} %param.8) | copy-start | bytes 6148
  9.2 83.7 %collective-permute-start = (bf16[3,32,64,512]{3,2,1,0:T(8,128)(2,1)}, bf16[3,32,64,512]{3,2,1,0:T(8,128)(2,1)S(1)}, u32[]{:S(2)}, u32[]{:S(2)}) collective-permute-start(bf16[3,32,64,512]{3,2,1,0:T(8,128)(2,1)} %bitcast.9), channel_id=1, source_target_pairs={{0,8},{8,0},{1,9},{9,1},{2,10},{10,2},{3,11},{11,3},{4,12},{12,4},... | collective-permute-start | bytes 18874376 | tf_op jit(solution)/shard_map/ppermute | solution.py:387
  9.3 83.6 %slice-start = ((s8[6291456]{0:T(1024)(128)(4,1)}), s8[4194304]{0:T(1024)(128)(4,1)S(1)}, s32[]{:S(2)}) async-start(s8[6291456]{0:T(1024)(128)(4,1)} %bitcast.10), calls=%async_computation.3 | async-start | bytes 8388608
  49.5 43.4 %slice-start.1 = ((s8[6291456]{0:T(1024)(128)(4,1)}), s8[2097152]{0:T(1024)(128)(4,1)S(1)}, s32[]{:S(2)}) async-start(s8[6291456]{0:T(1024)(128)(4,1)} %bitcast.10), calls=%async_computation.4 | async-start | bytes 4194304

commit v9 on v7

--- a/solution.py
+++ b/solution.py
@@ -70,18 +70,18 @@
         for half in range(2):
             acc = None
             for m in range(3):
-                rows = w_ref[m, :, 32 * half : 32 * half + 32, :].reshape(256, 512)
+                rows = w_ref[m, :, 32 * half : 32 * half + 32, :].reshape(512, 512)
                 term = lax.dot_general(
                     r_ref[m], rows, (((1,), (1,)), ((), ())), preferred_element_type=F32
                 )
                 acc = term if acc is None else acc + term
-            x_ref[step % 2, half] = acc.reshape(16, 32, 256)
+            x_ref[step % 2, half] = acc.reshape(16, 32, 512)
 
     def send():
         old = (step + 1) % 2
         for a_hi in range(16):
             h = a_hi ^ base
-            for tile in range(2):
+            for tile in range(4):
                 lanes = slice(128 * tile, 128 * tile + 128)
                 values = []
                 for t in range(4):
@@ -91,23 +91,23 @@
                         top,
                     )
                 for k, value in enumerate(butterfly(values, masks)):
-                    g = k ^ (2 * (step - 1) + tile)
+                    g = k ^ (4 * (step - 1) + tile)
                     out_ref[8 * h + g, :, lanes] = value.astype(BF16)
 
-    in_turn(step, multiply, send)
-
-
-def in_turn(step, first, second):
+    in_turn(step, 2, multiply, send)
+
+
+def in_turn(step, count, first, second):
     @pl.when(step == 0)
     def _():
         first()
 
-    @pl.when((step > 0) & (step < 4))
+    @pl.when((step > 0) & (step < count))
     def _():
         second()
         first()
 
-    @pl.when(step == 4)
+    @pl.when(step == count)
     def _():
         second()
 
@@ -115,15 +115,15 @@
 def make_cubes(r_pairs, w, shift):
     return pl.pallas_call(
         cube_kernel,
-        grid=(5,),
+        grid=(3,),
         in_specs=[
             whole((3, 512, 512)),
-            pl.BlockSpec((3, 8, 64, 512), lambda s: (0, jnp.minimum(s, 3), 0, 0)),
+            pl.BlockSpec((3, 16, 64, 512), lambda s: (0, jnp.minimum(s, 1), 0, 0)),
             whole((1, 1)),
         ],
-        out_specs=pl.BlockSpec((128, 8, 256), lambda s: (0, 0, jnp.maximum(s - 1, 0))),
+        out_specs=pl.BlockSpec((128, 8, 512), lambda s: (0, 0, jnp.maximum(s - 1, 0))),
         out_shape=jax.ShapeDtypeStruct((128, 8, 1024), BF16),
-        scratch_shapes=[pltpu.VMEM((2, 2, 16, 32, 256), F32)],
+        scratch_shapes=[pltpu.VMEM((2, 2, 16, 32, 512), F32)],
         compiler_params=params(58 * 1024 * 1024),
         cost_estimate=pl.CostEstimate(
             flops=2 * 512 * 2048 * 1536, bytes_accessed=10 * 1024**2, transcendentals=0
@@ -318,7 +318,7 @@
             )
             sum_ref[m] = term + jnp.where(step > 1, sum_ref[m], 0.0)
 
-    in_turn(step, receive, multiply)
+    in_turn(step, 4, receive, multiply)
 
     @pl.when(step == 4)
     def _():

time: 122 us -> 122 us (level)
  no operation moved by 1% of the time
where the time goes in v9:
time: 122 us; the launch traced here: 121 us
  blocking collectives  95.4 us (78%)
  Pallas kernels  25 us (20%)
    all_to_all x3, blocking collectives, exchange(): return lax.all_to_all(x, axis, split_axis=0, concat_axis=0, tiled=True)  95.4 us
    pallas_call x1, Pallas kernels, combine_at_owner(): pl.pallas_call(owner_kernel, in_specs=[SMEM_SPEC] + [VMEM_SPEC] * 5, out_...  9.41 us
    pallas_call x1, Pallas kernels, make_cubes(): pl.pallas_call(cube_kernel, grid=(3,), in_specs=[whole((3, 512, 512)), pl...  8.5 us
    pallas_call x1, Pallas kernels, contract(): pl.pallas_call(contract_kernel, grid=(5,), in_specs=[pl.BlockSpec((128, 8...  6.32 us
  transfers between devices with their start and end apart: 1, of which 0 were waited for; matrix products, arithmetic and copies ran while one was open for 0% of the time, Pallas kernels for 8%

profile of v9, /device:TPU:0, one launch (start us, length us, event | category | flops | bytes accessed | tf_op | source)
XLA Modules:
  0.0 121.3 jit_solution(1085916518261573727)
XLA Ops:
  0.7 8.5 %cubes.1 = bf16[128,8,1024]{2,1,0:T(8,128)(2,1)} custom-call(bf16[3,512,512]{2,1,0:T(8,128)(2,1)} %bitcast.16, bf16[3,32,64,512]{3,2,1,0:T(8,128)(2,1)} %bitcast.8, f32[1,1]{1,0:T(1,128)} %bitcast.6._), custom_call_target="tpu_custom_call" | custom-call | flops 3221225472 | bytes 10485760 | tf_op jit(solution)/shard_map/cubes/pallas_call | solution.py:116
  9.1 0.0 copy-start
  9.2 0.0 copy-start.1
  9.2 0.0 copy-start.2
  9.2 0.1 collective-permute-start
  9.3 0.0 slice-start
  9.3 40.2 %all_to_all.15.m_ref = bf16[128,8,1024]{2,1,0:T(8,128)(2,1)S(1)} all-to-all(bf16[128,8,1024]{2,1,0:T(8,128)(2,1)} %cubes.1), channel_id=1, replica_groups=mesh['xl'=2,'y'=4,'core'=2,'xh'=2,'z'=4] {'xl','y','core','xh','z'}, dimensions={0} | all-to-all | bytes 4194304 | tf_op jit(solution)/shard_map/all_to_all | solution.py:375
  49.5 0.0 copy-done
  49.5 0.0 copy-done.1
  49.5 0.0 copy-done.2
  49.5 0.0 slice-start.1
  49.5 9.4 %combine_at_owner.1 = bf16[128,8,1024]{2,1,0:T(8,128)(2,1)S(1)} custom-call(f32[4,128]{1,0:T(4,128)S(1)} %bitcast.14, f32[4,128]{1,0:T(4,128)S(1)} %bitcast.15, f32[1,1]{1,0:T(1,128)} %bitcast.7.shift_ref, bf16[128,8,1024]{2,1,0:T(8,128)(2,1)S(1)} %all_to_all.15.m_ref, bf16[1024,1024]{1,0:T(8,128)(2,1)S(1)} %copy-done, bf16[512,512]{1,0:T(8,128)(2,1)S(1)} %copy-done.1), custom_call_target="tpu_custom_call" | custom-call | tf_op jit(solution)/shard_map/combine_at_owner/pallas_call | solution.py:259
  58.9 34.2 %all_to_all.16.m_ref = bf16[128,8,1024]{2,1,0:T(8,128)(2,1)S(1)} all-to-all(bf16[128,8,1024]{2,1,0:T(8,128)(2,1)S(1)} %combine_at_owner.1), channel_id=1, replica_groups=mesh['xl'=2,'y'=4,'core'=2,'xh'=2,'z'=4] {'xl','y','core','xh','z'}, dimensions={0} | all-to-all | bytes 4194304 | tf_op jit(solution)/shard_map/all_to_all | solution.py:375
  93.1 0.0 collective-permute-done.other_ref
  93.1 0.0 slice-done
  93.1 0.0 slice-done.1
  93.1 6.3 %contract.1 = bf16[8,8,48,128]{3,2,1,0:T(8,128)(2,1)S(1)} custom-call(bf16[128,8,1024]{2,1,0:T(8,128)(2,1)S(1)} %all_to_all.16.m_ref, bf16[3,32,64,512]{3,2,1,0:T(8,128)(2,1)S(1)} %bitcast.12, bf16[3,32,64,512]{3,2,1,0:T(8,128)(2,1)S(1)} %collective-permute-done.other_ref), custom_call_target="tpu_custom_call" | custom-call | tf_op jit(solution)/shard_map/contract/pallas_call | solution.py:340
  99.5 21.0 %all_to_all.17.parts_ref = bf16[64,48,128]{2,1,0:T(8,128)(2,1)S(1)} all-to-all(bf16[64,48,128]{2,1,0:T(8,128)(2,1)S(1)} %bitcast.13), channel_id=1, replica_groups=mesh['xl'=2,'y'=4,'core'=2,'xh'=2,'z'=4] {'xl','y','xh','z'}, dimensions={0} | all-to-all | bytes 1572864 | tf_op jit(solution)/shard_map/all_to_all | solution.py:375
  120.5 0.8 total.1
  (1 shorter events, 0.0 us)
Async XLA Ops:
  9.1 40.3 %copy-start = (bf16[1024,1024]{1,0:T(8,128)(2,1)S(1)}, bf16[1024,1024]{1,0:T(8,128)(2,1)}, u32[]{:S(2)}) copy-start(bf16[1024,1024]{1,0:T(8,128)(2,1)} %constant.4.clone.perm_ref) | copy-start | bytes 6291460
  9.2 40.3 %copy-start.1 = (bf16[512,512]{1,0:T(8,128)(2,1)S(1)}, bf16[512,512]{1,0:T(8,128)(2,1)}, u32[]{:S(2)}) copy-start(bf16[512,512]{1,0:T(8,128)(2,1)} %constant.5.clone.turn_ref) | copy-start | bytes 1572868
  9.2 40.3 %copy-start.2 = (f32[512]{0:T(512)S(1)}, f32[512]{0:T(512)}, u32[]{:S(2)}) copy-start(f32[512]{0:T(512)} %param.8) | copy-start | bytes 6148
  9.2 84.0 %collective-permute-start = (bf16[3,32,64,512]{3,2,1,0:T(8,128)(2,1)}, bf16[3,32,64,512]{3,2,1,0:T(8,128)(2,1)S(1)}, u32[]{:S(2)}, u32[]{:S(2)}) collective-permute-start(bf16[3,32,64,512]{3,2,1,0:T(8,128)(2,1)} %bitcast.9), channel_id=1, source_target_pairs={{0,8},{8,0},{1,9},{9,1},{2,10},{10,2},{3,11},{11,3},{4,12},{12,4},... | collective-permute-start | bytes 18874376 | tf_op jit(solution)/shard_map/ppermute | solution.py:382
  9.3 83.9 %slice-start = ((s8[6291456]{0:T(1024)(128)(4,1)}), s8[4194304]{0:T(1024)(128)(4,1)S(1)}, s32[]{:S(2)}) async-start(s8[6291456]{0:T(1024)(128)(4,1)} %bitcast.10), calls=%async_computation.3 | async-start | bytes 8388608
  49.5 43.6 %slice-start.1 = ((s8[6291456]{0:T(1024)(128)(4,1)}), s8[2097152]{0:T(1024)(128)(4,1)S(1)}, s32[]{:S(2)}) async-start(s8[6291456]{0:T(1024)(128)(4,1)} %bitcast.10), calls=%async_computation.4 | async-start | bytes 4194304
